TPU v7x, 32 devices: a whole 2x2x4 slice. The times are simulated.
32 devices in a mesh: branch: 2 (over core), seq: 8 (over z, y), fsdp: 2 (over x).
Axes of the slice: x: 2, y: 2, z: 4, core: 2. Of those that a mesh axis runs over, the one named last changes fastest.
Arguments:
- latents: bfloat16 [1536, 5120], P('seq'), may hold values from -6 to 6
- noise: bfloat16 [2, 1536, 5120], P(None, 'seq'), may hold values from -6 to 6
- time_index: int32 [2], replicated, may hold values from 20 to 979
- cfg_pair: int32 [2], replicated, may hold values from 0 to 15
- cond_table: float32 [16, 5120], replicated, may hold values from -6 to 6
- gain: float32 [2, 5120], P('branch'), may hold values from 0.5 to 1.5
- w_qkv: bfloat16 [2, 3, 5120, 3072], P('branch', None, 'seq', 'fsdp'), may hold values from -0.5 to 0.5
- w_out: bfloat16 [2, 3072, 5120], P('branch', 'fsdp', 'seq'), may hold values from -0.109375 to 0.109375
Outputs:
- dmd_grad: float32 [1536, 5120], P('seq', ('branch', 'fsdp'))
- critic_residual: float32 [1536, 5120], P('seq', ('branch', 'fsdp'))
All inputs are finite; a program needn't handle non-finite values.
Results may differ from a plain program's by a relative error of at most 0.013.
Values may be sent and summed in bfloat16 or wider, within the bound.
No kernel may reach another device: no remote copies, remote signals or barrier semaphores. Data moves between devices by JAX's collectives and lax.ppermute only.
A program may use at most 128 MiB of HBM per device.

v0:
```python
import functools
import math

import jax
import jax.numpy as jnp
from jax import lax
from jax.experimental import pallas as pl
from jax.experimental.pallas import tpu as pltpu
from jax.sharding import Mesh
from jax.sharding import PartitionSpec as P


HD = 128
GUIDANCE = 3.5
EPSILON = 1e-06


def sigma_of(step_index):
    fraction = step_index.astype(jnp.float32) / 1000.0
    return 5.0 * fraction / (1.0 + 4.0 * fraction)


def noisy_mix(tokens, noise_rows, step_index):
    noise_level = sigma_of(step_index)
    return (1.0 - noise_level) * tokens + noise_level * noise_rows.astype(jnp.float32)


def table_row(cond_table, cond_row):
    one_hot = (jnp.arange(cond_table.shape[0], dtype=jnp.int32) == cond_row).astype(jnp.float32)
    return jnp.dot(one_hot, cond_table, precision=lax.Precision.HIGHEST)


def swap(x, axis):
    return lax.ppermute(x, axis, [(0, 1), (1, 0)])


def shift(x, axis, distance):
    size = lax.axis_size(axis)
    return lax.ppermute(x, axis, [(i, (i + distance) % size) for i in range(size)])


def prepare_kernel(b_ref, at_ref, time_ref, latents_ref, noise_ref, *refs):
    *out_refs, held_ref = refs
    _, width = latents_ref.shape
    blocks = at_ref.shape[0]
    step = jnp.full((1, HD), time_ref[b_ref[0]], jnp.int32)
    level = sigma_of(step)[:, :1]
    noisy = (1.0 - level) * latents_ref[...].astype(jnp.float32)
    noisy += level * noise_ref[0].astype(jnp.float32)
    mean_square = jnp.mean(noisy * noisy, axis=1, keepdims=True)
    held_ref[...] = noisy * lax.rsqrt(mean_square + EPSILON)
    size = width // blocks
    each = blocks // len(out_refs)
    for p in range(blocks):
        at = pl.multiple_of(at_ref[p] * size, HD)
        to = slice(p % each * size, (p % each + 1) * size)
        out_refs[p // each][:, to] = held_ref[:, pl.ds(at, size)].astype(jnp.bfloat16)


def prepare(b, order, time_index, latents, noise):
    tok, width = latents.shape
    tile = tok // 2 if tok % 32 == 0 else tok
    rows = pl.BlockSpec((tile, width), lambda t, *_: (t, 0))
    return pl.pallas_call(
        prepare_kernel,
        name="prepare",
        grid_spec=pltpu.PrefetchScalarGridSpec(
            num_scalar_prefetch=3,
            grid=(tok // tile,),
            in_specs=[rows, pl.BlockSpec((1, tile, width), lambda t, b, *_: (b[0], t, 0))],
            out_specs=[pl.BlockSpec((tile, width // 2), lambda t, *_: (t, 0))] * 2,
            scratch_shapes=[pltpu.VMEM((tile, width), jnp.float32)],
        ),
        out_shape=[jax.ShapeDtypeStruct((tok, width // 2), jnp.bfloat16)] * 2,
        cost_estimate=pl.CostEstimate(
            flops=6 * tok * width, transcendentals=tok, bytes_accessed=6 * tok * width
        ),
    )(b, order, time_index, latents, noise)


def affine_kernel(b_ref, at_ref, cfg_ref, own_ref, main_ref, gain_ref, table_ref, o_ref):
    b = b_ref[0]
    gain_row = gain_ref[...]
    own = own_ref[...]
    main = jnp.where(b == 0, own, main_ref[...]).astype(jnp.float32)
    cond = table_ref[pl.ds(cfg_ref[0], 1), :]
    second = table_ref[pl.ds(cfg_ref[1 - b], 1), :]
    o_ref[0] = (main * gain_row + cond).astype(jnp.bfloat16)
    o_ref[1] = (own.astype(jnp.float32) * gain_row + second).astype(jnp.bfloat16)


def affine(b, order, cfg_pair, own_rows, main_rows, gain, table):
    rows, width = own_rows.shape
    blocks = order.shape[0]
    size = width // blocks
    table = table.astype(jnp.float32)
    block = pl.BlockSpec((rows, size), lambda p, *_: (0, p))
    return pl.pallas_call(
        affine_kernel,
        name="affine",
        grid_spec=pltpu.PrefetchScalarGridSpec(
            num_scalar_prefetch=3,
            grid=(blocks,),
            in_specs=[
                block,
                block,
                pl.BlockSpec((1, size), lambda p, b, at, cfg: (0, at[p])),
                pl.BlockSpec((table.shape[0], size), lambda p, b, at, cfg: (0, at[p])),
            ],
            out_specs=pl.BlockSpec((2, rows, size), lambda p, *_: (0, 0, p)),
        ),
        out_shape=jax.ShapeDtypeStruct((2, rows, width), jnp.bfloat16),
        cost_estimate=pl.CostEstimate(
            flops=4 * rows * width, transcendentals=0, bytes_accessed=8 * rows * width
        ),
    )(b, order, cfg_pair, own_rows, main_rows, gain, table)


def project_kernel(place_ref, mine_ref, theirs_ref, *refs):
    blocks, (q_ref, kv_ref) = refs[:-2], refs[-2:]
    total = None
    for d in range(len(blocks) // 2):
        pair = blocks[2 * d : 2 * d + 2]
        weight = jnp.concatenate(
            [jnp.concatenate([w[j] for j in range(3)], axis=1) for w in pair], axis=0
        )
        depth = weight.shape[0]
        each = mine_ref.shape[2] // depth
        here = pl.ds(pl.multiple_of(place_ref[d] % each * depth, HD), depth)
        rows = jnp.where(place_ref[d] < each, mine_ref[0, :, here], theirs_ref[0, :, here])
        part = jnp.dot(rows, weight, preferred_element_type=jnp.float32)
        total = part if total is None else total + part
    total = total.astype(jnp.bfloat16)
    q_ref[0] = total[:, :HD]
    kv_ref[0] = total[:, HD:]


def project(mine, theirs, places, weights, own_swapped, pieces, head):
    passes, rows, half = mine.shape
    width = 2 * half
    depth = weights.shape[1]
    tile = rows // 2 if rows % 32 == 0 else rows
    whole = pl.BlockSpec((3, depth, HD), lambda p, t, at: (0, 0, 0))
    return pl.pallas_call(
        project_kernel,
        name="project",
        grid_spec=pltpu.PrefetchScalarGridSpec(
            num_scalar_prefetch=1,
            grid=(passes, rows // tile),
            in_specs=[
                pl.BlockSpec((1, tile, half), lambda p, t, at: (p, t, 0)),
                pl.BlockSpec((1, tile, half), lambda p, t, at: (p, t, 0)),
                pl.BlockSpec((3, depth, HD), lambda p, t, at: (0, 0, at[at.shape[0] - 1] + head)),
                pl.BlockSpec((3, depth, HD), lambda p, t, at: (0, 0, head)),
            ]
            + [whole] * len(pieces),
            out_specs=[
                pl.BlockSpec((1, tile, HD), lambda p, t, at: (p, t, 0)),
                pl.BlockSpec((1, tile, 2 * HD), lambda p, t, at: (p, t, 0)),
            ],
        ),
        out_shape=[
            jax.ShapeDtypeStruct((passes, rows, HD), jnp.bfloat16),
            jax.ShapeDtypeStruct((passes, rows, 2 * HD), jnp.bfloat16),
        ],
        cost_estimate=pl.CostEstimate(
            flops=6 * passes * rows * width * HD,
            transcendentals=0,
            bytes_accessed=2 * (passes * rows * (width + 3 * HD) + 3 * width * HD),
        ),
    )(places, mine, theirs, weights, own_swapped, *pieces)


def attend_kernel(b_ref, q_ref, own_ref, other_ref, o_ref, give_ref):
    dims = (((1,), (1,)), ((), ()))
    scale = HD ** (-0.5)
    tile = q_ref.shape[1]
    step, steps = pl.program_id(0), pl.num_programs(0)
    mixed = []
    for p in range(2):
        q, own, other = q_ref[p], own_ref[p], other_ref[p]
        s0 = lax.dot_general(q, own[:, :HD], dims, preferred_element_type=jnp.float32) * scale
        s1 = lax.dot_general(q, other[:, :HD], dims, preferred_element_type=jnp.float32) * scale
        peak = jnp.maximum(
            jnp.max(s0, axis=1, keepdims=True), jnp.max(s1, axis=1, keepdims=True)
        )
        p0 = jnp.exp(s0 - peak)
        p1 = jnp.exp(s1 - peak)
        mass = jnp.sum(p0, axis=1, keepdims=True) + jnp.sum(p1, axis=1, keepdims=True)
        total = jnp.dot(p0.astype(jnp.bfloat16), own[:, HD:], preferred_element_type=jnp.float32)
        total += jnp.dot(
            p1.astype(jnp.bfloat16), other[:, HD:], preferred_element_type=jnp.float32
        )
        mixed.append(total / mass)
    teacher = b_ref[0] == 0
    main = jnp.where(teacher, mixed[1] + GUIDANCE * (mixed[0] - mixed[1]), mixed[0])
    second = mixed[1].astype(jnp.bfloat16)
    o_ref[pl.ds(step * tile, tile), :] = main.astype(jnp.bfloat16)

    @pl.when(step < steps // 2)
    def _():
        give_ref[pl.ds(step * tile, tile), :] = second

    @pl.when(step >= steps // 2)
    def _():
        o_ref[pl.ds((step + steps // 2) * tile, tile), :] = second


def attend(b, q, own, other):
    passes, rows, _ = q.shape
    keys = own.shape[1] + other.shape[1]
    tile = rows // 4 if rows % 64 == 0 else rows // 2
    kv_spec = pl.BlockSpec((passes, own.shape[1], 2 * HD), lambda t, b: (0, 0, 0))
    return pl.pallas_call(
        attend_kernel,
        name="attend",
        grid_spec=pltpu.PrefetchScalarGridSpec(
            num_scalar_prefetch=1,
            grid=(rows // tile,),
            in_specs=[
                pl.BlockSpec((passes, tile, HD), lambda t, b: (0, t, 0)),
                kv_spec,
                kv_spec,
            ],
            out_specs=[
                pl.BlockSpec((rows * 3 // 2, HD), lambda t, b: (0, 0)),
                pl.BlockSpec((rows // 2, HD), lambda t, b: (0, 0)),
            ],
        ),
        out_shape=[
            jax.ShapeDtypeStruct((rows * 3 // 2, HD), jnp.bfloat16),
            jax.ShapeDtypeStruct((rows // 2, HD), jnp.bfloat16),
        ],
        cost_estimate=pl.CostEstimate(
            flops=4 * passes * rows * keys * HD,
            transcendentals=passes * rows * keys,
            bytes_accessed=2 * (2 * q.size + 2 * own.size),
        ),
    )(b, q, own, other)


def project_out_kernel(count, first, at_ref, *refs):
    pieces, weights, refs = refs[:count], refs[count : 2 * count], refs[2 * count :]
    rows = jnp.concatenate([a[...] for a in pieces], axis=1)
    weight = jnp.concatenate([w[0] for w in weights], axis=0)
    total = jnp.dot(rows, weight, preferred_element_type=jnp.float32)
    refs[-1][...] = total if first else refs[0][...] + total


def project_out(sets, tiles, places, mine, theirs, carry):
    tile = sets[0][1][0].shape[0] // 3
    each = len(sets[0][1]) // 2
    count = 2 * each * len(sets)
    width = mine.shape[2]
    lo, hi = tiles
    rows = (hi - lo) * tile
    first = carry is None

    def weight_spec(k, head):
        return pl.BlockSpec((1, HD, width), lambda t, at: ((t + lo) // 2, at[k] + head, 0))

    return pl.pallas_call(
        functools.partial(project_out_kernel, count, first),
        name="project_out",
        grid_spec=pltpu.PrefetchScalarGridSpec(
            num_scalar_prefetch=1,
            grid=(hi - lo,),
            in_specs=[pl.BlockSpec((tile, HD), lambda t, at: (t + lo, 0))] * count
            + [weight_spec(k % each, head) for head, _ in sets for k in range(2 * each)]
            + ([] if first else [pl.BlockSpec((tile, width), lambda t, at: (t + lo, 0))]),
            out_specs=pl.BlockSpec((tile, width), lambda t, at: (t, 0)),
        ),
        out_shape=jax.ShapeDtypeStruct((rows, width), jnp.float32),
        cost_estimate=pl.CostEstimate(
            flops=2 * rows * width * HD * count,
            transcendentals=0,
            bytes_accessed=2 * HD * count * (rows + width) + 8 * rows * width,
        ),
    )(
        places,
        *[piece for _, pieces in sets for piece in pieces],
        *(([mine] * each + [theirs] * each) * len(sets)),
        *([] if first else [carry]),
    )


def split_body(*operands):
    return split_step(*operands)


def split_step(latents, noise, time_index, cfg_pair, cond_table, gain, w_qkv, w_out):
    b = lax.axis_index("branch")
    z = lax.axis_index("outer")
    y = lax.axis_index("inner")
    f = lax.axis_index("fsdp")
    nz = lax.axis_size("outer")
    nf = lax.axis_size("fsdp")
    tok, width = latents.shape
    half = width // nf
    weights = w_qkv[0]
    _, cols = weights.shape[1:]
    head_count = cols // HD // nz

    span = head_count * HD
    own_swapped = swap(lax.dynamic_slice_in_dim(weights, z * span, span, 2), "inner")
    head_pieces = []
    for head in range(head_count):
        pieces = []
        for d in range(1, nz):
            start = (z + d) % nz * span + head * HD
            send = lax.dynamic_slice_in_dim(weights, start, HD, 2)
            received = shift(send, "outer", d)
            pieces += [received, swap(received, "inner")]
        head_pieces.append(pieces)
    from_z = jnp.stack([(z - d) % nz for d in range(nz)])
    places = jnp.concatenate([(from_z - 2 * f) % nz, (z * head_count)[None]]).astype(jnp.int32)

    which = b[None].astype(jnp.int32)
    order = jnp.stack(
        [(p // 2 + f * (nz // nf)) % nz * 2 + (y ^ (p % 2)) for p in range(2 * nz)]
    ).astype(jnp.int32)
    unit = prepare(which, order, time_index, latents, noise)
    ups = downs = [(unit[0], None)]
    for k in range(1, nz):
        up = lax.ppermute(ups[-1][0], "outer", [(i, i + 1) for i in range(k - 1, nz - 1)])
        down = lax.ppermute(downs[-1][0], "outer", [(i, i - 1) for i in range(1, nz - k + 1)])
        pairs = [(i * nf + j, i * nf + 1 - j) for i in range(nz) for j in range(nf)]
        ups = ups + [(up, lax.ppermute(up, ("outer", "fsdp"), pairs[k * nf :]))]
        downs = downs + [(down, lax.ppermute(down, ("outer", "fsdp"), pairs[: -k * nf]))]
    inputs = []
    for side in range(2):
        own_rows = jnp.zeros((nz * tok, half), jnp.bfloat16)
        own_rows = lax.dynamic_update_slice(own_rows, unit[side], (z * tok, 0))
        for k in range(1, nz):
            block = jnp.where(z + k < nz, downs[k][side], ups[nz - k][side])
            own_rows = lax.dynamic_update_slice(own_rows, block, ((z + k) % nz * tok, 0))
        main_rows = lax.ppermute(own_rows, "branch", [(0, 1)])
        part = order[side * nz : (side + 1) * nz]
        inputs.append(affine(which, part, cfg_pair, own_rows, main_rows, gain, cond_table))

    out_here = w_out[0]
    out_width = out_here.shape[1]
    out_there = swap(out_here, "inner")
    out_mine = jnp.where(f == y, out_here, out_there)
    out_theirs = swap(jnp.where(f == y, out_there, out_here), "fsdp")
    out_own = jnp.stack([out_mine, out_theirs])
    out_critic = lax.ppermute(out_own, "branch", [(1, 0)])
    out_critic = jnp.where(b == 0, out_critic, out_own)
    out_pairs = jnp.stack([out_own, out_critic], axis=1)
    out_mine, out_theirs = out_pairs[0], out_pairs[1]
    out_places = (from_z * head_count).astype(jnp.int32)

    rows = nz * tok
    sets = []
    for head in range(head_count):
        q, pair = project(*inputs, places, weights, own_swapped, head_pieces[head], head)
        other = swap(pair, "inner")
        attn, give = attend(which, q, pair, other)
        taken = lax.ppermute(give, "branch", [(1, 0)])
        attn = lax.dynamic_update_slice(attn, jnp.where(b == 0, taken, attn[rows:]), (rows, 0))
        ours, across = [attn], [swap(attn, "fsdp")]
        for _ in range(1, nz):
            ours.append(shift(ours[-1], "outer", 1))
            across.append(swap(ours[-1], "fsdp"))
        sets.append((head, ours + across))
    last = (out_places, out_mine, out_theirs)
    early = project_out(sets[:-1], (0, 3), *last, None)
    pred = project_out(sets[-1:], (0, 2), *last, early)
    own_pred = project_out(sets[-1:], (2, 3), *last, early)

    kept = lax.dynamic_slice_in_dim(pred, b * (rows // 2), rows // 2, 0)
    given = lax.dynamic_slice_in_dim(pred, (1 - b) * (rows // 2), rows // 2, 0)
    given = swap(given, "branch")
    dmd = jnp.where(b == 0, given - kept, kept - given)
    value = jnp.stack([dmd, own_pred]).astype(jnp.bfloat16)
    value = value.reshape(2, nz // 2, tok, out_width)
    received = []
    axes = ("branch", "outer", "fsdp")
    for k in range(nz // 2):
        pairs = []
        for bb in range(2):
            for zz in range(nz):
                for ff in range(nf):
                    to = bb * (nz // 2) + (ff + k) % (nz // 2)
                    source = (bb * nz + zz) * nf + ff
                    target = (zz // nf * nz + to) * nf + zz % nf
                    pairs.append((source, target))
        block = lax.dynamic_index_in_dim(value, (f + k) % (nz // 2), 1, keepdims=False)
        received.append(lax.ppermute(block, axes, pairs))
    swapped = z % (nz // 2) == 1
    first = jnp.where(swapped, received[1], received[0])
    second = jnp.where(swapped, received[0], received[1])
    done = jnp.concatenate([first, second], axis=2).astype(jnp.float32)
    out_cols = out_width * nf
    col_start = (b * nf + f) * out_cols
    noise_cols = lax.dynamic_slice_in_dim(noise[1], col_start, out_cols, 1).astype(jnp.float32)
    latent_cols = lax.dynamic_slice_in_dim(latents, col_start, out_cols, 1).astype(jnp.float32)
    return (done[0], done[1] - (noise_cols - latent_cols))


def attend_all(queries, key_rows, value_rows):
    passes, key_count = (key_rows.shape[0], key_rows.shape[1])
    local_heads = queries.shape[2]
    key_rows = key_rows.reshape(passes, key_count, local_heads, HD)
    value_rows = value_rows.reshape(passes, key_count, local_heads, HD)
    scores = jnp.einsum(
        "pqhd,prhd->pqhr", queries, key_rows, preferred_element_type=jnp.float32
    ) * HD ** (-0.5)
    softmax_w = jnp.exp(scores - jnp.max(scores, axis=-1, keepdims=True))
    mass = jnp.sum(softmax_w, axis=-1)
    mixed = jnp.einsum(
        "pqhr,prhd->pqhd",
        softmax_w.astype(jnp.bfloat16),
        value_rows,
        preferred_element_type=jnp.float32,
    )
    return (mixed / mass[..., None]).astype(jnp.bfloat16)


def normed(noisy_rows, gain_row, shift_row):
    mean_square = jnp.mean(noisy_rows * noisy_rows, axis=-1, keepdims=True)
    return (noisy_rows * lax.rsqrt(mean_square + EPSILON) * gain_row + shift_row).astype(
        jnp.bfloat16
    )


def gathered_body(latents, noise, time_index, cfg_pair, cond_table, gain, w_qkv, w_out):
    branch = lax.axis_index("branch")
    fsdp_count = lax.axis_size("fsdp")
    tok_rows = latents.shape[0]
    tokens = latents.astype(jnp.float32)
    noisy_main = noisy_mix(tokens, noise[0], time_index[0])
    own_noise = lax.dynamic_index_in_dim(noise, branch, 0, keepdims=False)
    own_index = lax.dynamic_index_in_dim(time_index, branch, 0, keepdims=False)
    noisy_own = noisy_mix(tokens, own_noise, own_index)
    cond_shift = table_row(cond_table, cfg_pair[0])
    second_row = lax.dynamic_index_in_dim(cfg_pair, 1 - branch, 0, keepdims=False)
    second_shift = table_row(cond_table, second_row)
    gain_row = gain[0]
    inputs = jnp.stack(
        [normed(noisy_main, gain_row, cond_shift), normed(noisy_own, gain_row, second_shift)]
    )
    weights = w_qkv[0]
    col_count = weights.shape[2]
    local_heads = col_count // HD
    projected = jnp.einsum(
        "ptd,jdc->pjtc",
        inputs,
        lax.all_gather(weights, "seq", axis=1, tiled=True),
        preferred_element_type=jnp.float32,
    ).astype(jnp.bfloat16)
    attn = attend_all(
        projected[:, 0].reshape(2, tok_rows, local_heads, HD),
        lax.all_gather(projected[:, 1], "seq", axis=1, tiled=True),
        lax.all_gather(projected[:, 2], "seq", axis=1, tiled=True),
    ).reshape(2, tok_rows, col_count)
    partial_value = jnp.einsum(
        "ptc,cd->ptd",
        attn,
        lax.all_gather(w_out[0], "seq", axis=1, tiled=True),
        preferred_element_type=jnp.float32,
    )
    width_all = partial_value.shape[2]
    half_width = width_all // (2 * fsdp_count)
    partial_value = (
        partial_value.reshape(2, tok_rows, 2, fsdp_count, half_width)
        .transpose(0, 1, 3, 2, 4)
        .reshape(2, tok_rows, width_all)
    )
    head_sums = lax.psum_scatter(
        partial_value.astype(jnp.bfloat16), "fsdp", scatter_dimension=2, tiled=True
    ).astype(jnp.float32)
    own_half = lax.dynamic_slice_in_dim(head_sums, branch * half_width, half_width, 2)
    give_half = lax.dynamic_slice_in_dim(head_sums, (1 - branch) * half_width, half_width, 2)
    partner_half = swap(give_half.astype(jnp.bfloat16), "branch").astype(jnp.float32)
    is_teacher = branch == 0
    teacher = jnp.where(is_teacher, own_half, partner_half)
    critic = jnp.where(is_teacher, partner_half, own_half)
    dmd_grad = critic[0] - (teacher[1] + GUIDANCE * (teacher[0] - teacher[1]))
    col_start = (branch * fsdp_count + lax.axis_index("fsdp")) * half_width
    noise_cols = lax.dynamic_slice_in_dim(noise[1], col_start, half_width, 1).astype(jnp.float32)
    latent_cols = lax.dynamic_slice_in_dim(latents, col_start, half_width, 1).astype(jnp.float32)
    return (dmd_grad, critic[1] - (noise_cols - latent_cols))


def solution(mesh):
    sizes = dict(mesh.shape)
    branches, seq, fsdp = sizes["branch"], sizes["seq"], sizes["fsdp"]

    def run(latents, noise, time_index, cfg_pair, cond_table, gain, w_qkv, w_out):
        local_heads = w_qkv.shape[3] // HD // fsdp
        outer = math.gcd(local_heads, seq)
        split = outer == branches * fsdp and seq == 2 * outer and branches == 2 and fsdp == 2
        if split:
            used = Mesh(
                mesh.devices.reshape(branches, outer, 2, fsdp),
                ("branch", "outer", "inner", "fsdp"),
            )
            body, along = split_body, ("outer", "inner")
        else:
            used, body, along = mesh, gathered_body, "seq"
        out = P(along, ("branch", "fsdp"))
        step = jax.shard_map(
            body,
            mesh=used,
            in_specs=(
                P(along, None),
                P(None, along, None),
                P(),
                P(),
                P(),
                P("branch", None),
                P("branch", None, along, "fsdp"),
                P("branch", "fsdp", along),
            ),
            out_specs=(out, out),
            check_vma=False,
        )
        return step(latents, noise, time_index, cfg_pair, cond_table, gain, w_qkv, w_out)

    return run
```

profile of v0, /device:TPU:9, one launch (start us, length us, event | category | flops | bytes accessed | tf_op | source)
XLA Modules:
  0.0 573.0 jit_solution(13887311922657594791)
XLA Ops:
  11.4 19.5 %collective-permute-done.1 = bf16[192,2560]{1,0:T(8,128)(2,1)S(1)} collective-permute-done((bf16[192,2560]{1,0:T(8,128)(2,1)}, bf16[192,2560]{1,0:T(8,128)(2,1)S(1)}, u32[]{:S(2)}, u32[]{:S(2)}) %collective-permute-start.1) | collective-permute-done | bytes 983072 | tf_op jit(solution)/shard_map/ppermute | solution.py:325
  37.0 16.8 %collective-permute-done.2 = bf16[192,2560]{1,0:T(8,128)(2,1)} collective-permute-done((bf16[192,2560]{1,0:T(8,128)(2,1)S(1)}, bf16[192,2560]{1,0:T(8,128)(2,1)}, u32[]{:S(2)}, u32[]{:S(2)}) %collective-permute-start.2) | collective-permute-done | bytes 983072 | tf_op jit(solution)/shard_map/ppermute | solution.py:325
  72.5 14.1 %collective-permute-done.5 = bf16[192,2560]{1,0:T(8,128)(2,1)S(1)} collective-permute-done((bf16[192,2560]{1,0:T(8,128)(2,1)S(1)}, bf16[192,2560]{1,0:T(8,128)(2,1)S(1)}, u32[]{:S(2)}, u32[]{:S(2)}) %collective-permute-start.5) | collective-permute-done | bytes 983072 | tf_op jit(solution)/shard_map/ppermute | solution.py:326
  96.3 12.1 %collective-permute-done.9 = bf16[192,2560]{1,0:T(8,128)(2,1)S(1)} collective-permute-done((bf16[192,2560]{1,0:T(8,128)(2,1)S(1)}, bf16[192,2560]{1,0:T(8,128)(2,1)S(1)}, u32[]{:S(2)}, u32[]{:S(2)}) %collective-permute-start.9) | collective-permute-done | bytes 983072 | tf_op jit(solution)/shard_map/ppermute | solution.py:329
  109.5 19.9 %collective-permute-done.12 = bf16[192,2560]{1,0:T(8,128)(2,1)S(1)} collective-permute-done((bf16[192,2560]{1,0:T(8,128)(2,1)S(1)}, bf16[192,2560]{1,0:T(8,128)(2,1)S(1)}, u32[]{:S(2)}, u32[]{:S(2)}) %collective-permute-start.12) | collective-permute-done | bytes 983072 | tf_op jit(solution)/shard_map/ppermute | solution.py:328
  142.5 6.6 %collective-permute-done.52.refs_6_ = bf16[3,640,128]{2,1,0:T(8,128)(2,1)} collective-permute-done((bf16[3,640,128]{2,1,0:T(8,128)(2,1)S(1)}, bf16[3,640,128]{2,1,0:T(8,128)(2,1)}, u32[]{:S(2)}, u32[]{:S(2)}) %collective-permute-start.52) | collective-permute-done | bytes 491552 | tf_op jit(solution)/shard_map/ppermute | solution.py:39
  149.2 18.1 %collective-permute-done.48.refs_2_ = bf16[3,640,128]{2,1,0:T(8,128)(2,1)} collective-permute-done((bf16[3,640,128]{2,1,0:T(8,128)(2,1)S(1)}, bf16[3,640,128]{2,1,0:T(8,128)(2,1)}, u32[]{:S(2)}, u32[]{:S(2)}) %collective-permute-start.48) | collective-permute-done | bytes 491552 | tf_op jit(solution)/shard_map/ppermute | solution.py:39
  171.4 45.5 %collective-permute-done.35.refs_4_ = bf16[3,640,128]{2,1,0:T(8,128)(2,1)S(1)} collective-permute-done((bf16[3,640,128]{2,1,0:T(8,128)(2,1)S(1)}, bf16[3,640,128]{2,1,0:T(8,128)(2,1)S(1)}, u32[]{:S(2)}, u32[]{:S(2)}) %collective-permute-start.35) | collective-permute-done | bytes 491552 | tf_op jit(solution)/shard_map/ppermute | solution.py:39
  221.9 9.6 %collective-permute-done.17.refs_4_ = bf16[3,640,128]{2,1,0:T(8,128)(2,1)} collective-permute-done((bf16[3,640,128]{2,1,0:T(8,128)(2,1)}, bf16[3,640,128]{2,1,0:T(8,128)(2,1)}, u32[]{:S(2)}, u32[]{:S(2)}) %collective-permute-start.17) | collective-permute-done | bytes 491552 | tf_op jit(solution)/shard_map/ppermute | solution.py:39
  243.5 7.2 %collective-permute-start.32 = (bf16[2,1536,640]{2,1,0:T(8,128)(2,1)}, bf16[2,1536,640]{2,1,0:T(8,128)(2,1)}, u32[]{:S(2)}, u32[]{:S(2)}) collective-permute-start(bf16[2,1536,640]{2,1,0:T(8,128)(2,1)} %pad_maximum_fusion.1), channel_id=1, source_target_pairs={{16,0},{17,1},{18,2},{19,3},{20,4},{21,5},{22,6},{23,7},{24,8},{25... | collective-permute-start | bytes 11796488 | tf_op jit(solution)/shard_map/ppermute | solution.py:347
  250.7 11.9 %collective-permute-done.50.refs_4_ = bf16[3,640,128]{2,1,0:T(8,128)(2,1)} collective-permute-done((bf16[3,640,128]{2,1,0:T(8,128)(2,1)}, bf16[3,640,128]{2,1,0:T(8,128)(2,1)}, u32[]{:S(2)}, u32[]{:S(2)}) %collective-permute-start.50) | collective-permute-done | bytes 491552 | tf_op jit(solution)/shard_map/ppermute | solution.py:39
  265.6 8.2 %affine.2.mine_ref = bf16[2,768,2560]{2,1,0:T(8,128)(2,1)} custom-call(s32[1]{0:T(128)} %bitcast.4.b_ref, s32[4]{0:T(128)} %get-tuple-element.51.at_ref, s32[2]{0:T(128)} %cfg_ref.3, bf16[768,2560]{1,0:T(8,128)(2,1)} %select_dynamic-update-slice_fusion.3.own_ref, bf16[768,2560]{1,0:T(8,128)(2,1)} %collective-permute-done.6.main_ref, f32[1,5120]{1,0:T(1,128)} %gain_ref.3, ...), custom_call_target="tpu_custom_call" | custom-call | flops 7864320 | bytes 15728640 | tf_op jit(solution)/shard_map/affine/pallas_call | solution.py:98
  273.8 8.2 %affine.3.theirs_ref = bf16[2,768,2560]{2,1,0:T(8,128)(2,1)} custom-call(s32[1]{0:T(128)} %bitcast.4.b_ref, s32[4]{0:T(128)} %get-tuple-element.52.at_ref, s32[2]{0:T(128)} %cfg_ref.3, bf16[768,2560]{1,0:T(8,128)(2,1)} %select_dynamic-update-slice_fusion.own_ref, bf16[768,2560]{1,0:T(8,128)(2,1)} %collective-permute-done.13.main_ref, f32[1,5120]{1,0:T(1,128)} %gain_ref.3, ...), custom_call_target="tpu_custom_call" | custom-call | flops 7864320 | bytes 15728640 | tf_op jit(solution)/shard_map/affine/pallas_call | solution.py:98
  286.5 8.7 %collective-permute-done.51.refs_5_ = bf16[3,640,128]{2,1,0:T(8,128)(2,1)} collective-permute-done((bf16[3,640,128]{2,1,0:T(8,128)(2,1)}, bf16[3,640,128]{2,1,0:T(8,128)(2,1)}, u32[]{:S(2)}, u32[]{:S(2)}) %collective-permute-start.51) | collective-permute-done | bytes 491552 | tf_op jit(solution)/shard_map/ppermute | solution.py:34
  296.6 13.8 %project.5 = (bf16[2,768,128]{2,1,0:T(8,128)(2,1)}, bf16[2,768,256]{2,1,0:T(8,128)(2,1)}) custom-call(s32[5]{0:T(128)} %pad_add_fusion.1.place_ref, bf16[2,768,2560]{2,1,0:T(8,128)(2,1)} %affine.2.mine_ref, bf16[2,768,2560]{2,1,0:T(8,128)(2,1)} %affine.3.theirs_ref, bf16[3,640,1536]{2,1,0:T(8,128)(2,1)} %bitcast.66, bf16[3,640,384]{2,1,0:T(8,128)(2,1)} %copy-done.1, ...), custom_call_target="tpu_custom_call" | custom-call | flops 6039797760 | bytes 20840448 | tf_op jit(solution)/shard_map/project/pallas_call | solution.py:144
  316.4 10.3 %collective-permute-done.16.refs_3_ = bf16[3,640,128]{2,1,0:T(8,128)(2,1)} collective-permute-done((bf16[3,640,128]{2,1,0:T(8,128)(2,1)}, bf16[3,640,128]{2,1,0:T(8,128)(2,1)}, u32[]{:S(2)}, u32[]{:S(2)}) %collective-permute-start.16) | collective-permute-done | bytes 491552 | tf_op jit(solution)/shard_map/ppermute | solution.py:34
  327.0 13.6 %project.3 = (bf16[2,768,128]{2,1,0:T(8,128)(2,1)}, bf16[2,768,256]{2,1,0:T(8,128)(2,1)}) custom-call(s32[5]{0:T(128)} %pad_add_fusion.1.place_ref, bf16[2,768,2560]{2,1,0:T(8,128)(2,1)} %affine.2.mine_ref, bf16[2,768,2560]{2,1,0:T(8,128)(2,1)} %affine.3.theirs_ref, bf16[3,640,1536]{2,1,0:T(8,128)(2,1)} %bitcast.67, bf16[3,640,384]{2,1,0:T(8,128)(2,1)} %copy-done.1, ...), custom_call_target="tpu_custom_call" | custom-call | flops 6039797760 | bytes 20840448 | tf_op jit(solution)/shard_map/project/pallas_call | solution.py:144
  347.7 10.5 %collective-permute-done.34.refs_3_ = bf16[3,640,128]{2,1,0:T(8,128)(2,1)S(1)} collective-permute-done((bf16[3,640,128]{2,1,0:T(8,128)(2,1)}, bf16[3,640,128]{2,1,0:T(8,128)(2,1)S(1)}, u32[]{:S(2)}, u32[]{:S(2)}) %collective-permute-start.34) | collective-permute-done | bytes 491552 | tf_op jit(solution)/shard_map/ppermute | solution.py:34
  359.1 13.6 %project.4 = (bf16[2,768,128]{2,1,0:T(8,128)(2,1)}, bf16[2,768,256]{2,1,0:T(8,128)(2,1)}) custom-call(s32[5]{0:T(128)} %pad_add_fusion.1.place_ref, bf16[2,768,2560]{2,1,0:T(8,128)(2,1)} %affine.2.mine_ref, bf16[2,768,2560]{2,1,0:T(8,128)(2,1)} %affine.3.theirs_ref, bf16[3,640,1536]{2,1,0:T(8,128)(2,1)} %bitcast.68, bf16[3,640,384]{2,1,0:T(8,128)(2,1)} %copy-done.1, ...), custom_call_target="tpu_custom_call" | custom-call | flops 6039797760 | bytes 20840448 | tf_op jit(solution)/shard_map/project/pallas_call | solution.py:144
  376.0 7.7 %attend.5 = (bf16[1152,128]{1,0:T(8,128)(2,1)}, bf16[384,128]{1,0:T(8,128)(2,1)}) custom-call(s32[1]{0:T(128)} %bitcast.4.b_ref, bf16[2,768,128]{2,1,0:T(8,128)(2,1)} %get-tuple-element.26.q_ref, bf16[2,768,256]{2,1,0:T(8,128)(2,1)} %get-tuple-element.27.own_ref, bf16[2,768,256]{2,1,0:T(8,128)(2,1)} %copy-done.31), custom_call_target="tpu_custom_call" | custom-call | flops 1207959552 | bytes 2359296 | tf_op jit(solution)/shard_map/attend/pallas_call | solution.py:214
  383.7 6.5 %collective-permute-start.55 = (bf16[384,128]{1,0:T(8,128)(2,1)}, bf16[384,128]{1,0:T(8,128)(2,1)S(1)}, u32[]{:S(2)}, u32[]{:S(2)}) collective-permute-start(bf16[384,128]{1,0:T(8,128)(2,1)} %get-tuple-element.29), channel_id=1, source_target_pairs={{16,0},{17,1},{18,2},{19,3},{20,4},{21,5},{22,6},{23,7},{24,8},{25... | collective-permute-start | bytes 294920 | tf_op jit(solution)/shard_map/ppermute | solution.py:359
  392.1 7.9 %attend.3 = (bf16[1152,128]{1,0:T(8,128)(2,1)}, bf16[384,128]{1,0:T(8,128)(2,1)}) custom-call(s32[1]{0:T(128)} %bitcast.4.b_ref, bf16[2,768,128]{2,1,0:T(8,128)(2,1)} %get-tuple-element.18.q_ref, bf16[2,768,256]{2,1,0:T(8,128)(2,1)} %get-tuple-element.19.own_ref, bf16[2,768,256]{2,1,0:T(8,128)(2,1)} %collective-permute-done.21.other_ref), custom_call_target="tpu_custom_call" | custom-call | flops 1207959552 | bytes 2359296 | tf_op jit(solution)/shard_map/attend/pallas_call | solution.py:214
  399.9 6.6 %collective-permute-start.22 = (bf16[384,128]{1,0:T(8,128)(2,1)}, bf16[384,128]{1,0:T(8,128)(2,1)S(1)}, u32[]{:S(2)}, u32[]{:S(2)}) collective-permute-start(bf16[384,128]{1,0:T(8,128)(2,1)} %get-tuple-element.21), channel_id=1, source_target_pairs={{16,0},{17,1},{18,2},{19,3},{20,4},{21,5},{22,6},{23,7},{24,8},{25... | collective-permute-start | bytes 294920 | tf_op jit(solution)/shard_map/ppermute | solution.py:359
  408.9 7.7 %attend.4 = (bf16[1152,128]{1,0:T(8,128)(2,1)}, bf16[384,128]{1,0:T(8,128)(2,1)}) custom-call(s32[1]{0:T(128)} %bitcast.4.b_ref, bf16[2,768,128]{2,1,0:T(8,128)(2,1)} %get-tuple-element.22.q_ref, bf16[2,768,256]{2,1,0:T(8,128)(2,1)} %get-tuple-element.23.own_ref, bf16[2,768,256]{2,1,0:T(8,128)(2,1)} %collective-permute-done.39.other_ref), custom_call_target="tpu_custom_call" | custom-call | flops 1207959552 | bytes 2359296 | tf_op jit(solution)/shard_map/attend/pallas_call | solution.py:214
  442.4 6.4 %collective-permute-done.23.refs_1_ = bf16[1152,128]{1,0:T(8,128)(2,1)S(1)} collective-permute-done((bf16[1152,128]{1,0:T(8,128)(2,1)S(1)}, bf16[1152,128]{1,0:T(8,128)(2,1)S(1)}, u32[]{:S(2)}, u32[]{:S(2)}) %collective-permute-start.23) | collective-permute-done | bytes 294944 | tf_op jit(solution)/shard_map/ppermute | solution.py:39
  461.4 6.4 %collective-permute-done.24.refs_2_ = bf16[1152,128]{1,0:T(8,128)(2,1)S(1)} collective-permute-done((bf16[1152,128]{1,0:T(8,128)(2,1)S(1)}, bf16[1152,128]{1,0:T(8,128)(2,1)S(1)}, u32[]{:S(2)}, u32[]{:S(2)}) %collective-permute-start.24) | collective-permute-done | bytes 294944 | tf_op jit(solution)/shard_map/ppermute | solution.py:39
  477.5 8.9 %collective-permute-done.25.refs_3_ = bf16[1152,128]{1,0:T(8,128)(2,1)S(1)} collective-permute-done((bf16[1152,128]{1,0:T(8,128)(2,1)S(1)}, bf16[1152,128]{1,0:T(8,128)(2,1)S(1)}, u32[]{:S(2)}, u32[]{:S(2)}) %collective-permute-start.25) | collective-permute-done | bytes 294944 | tf_op jit(solution)/shard_map/ppermute | solution.py:39
  493.1 21.3 %collective-permute-done.47.refs_7_ = bf16[1152,128]{1,0:T(8,128)(2,1)S(1)} collective-permute-done((bf16[1152,128]{1,0:T(8,128)(2,1)S(1)}, bf16[1152,128]{1,0:T(8,128)(2,1)S(1)}, u32[]{:S(2)}, u32[]{:S(2)}) %collective-permute-start.47) | collective-permute-done | bytes 294944 | tf_op jit(solution)/shard_map/ppermute | solution.py:34
  515.2 9.4 %project_out.3.refs_16_ = f32[1152,640]{1,0:T(8,128)} custom-call(s32[4]{0:T(128)} %broadcast_multiply_fusion.at_ref, bf16[1152,128]{1,0:T(8,128)(2,1)} %select_dynamic-update-slice_fusion.7.refs_0_, bf16[1152,128]{1,0:T(8,128)(2,1)} %copy-done.24, bf16[1152,128]{1,0:T(8,128)(2,1)} %collective-permute-done.42.refs_2_, bf16[1152,128]{1,0:T(8,128)(2,1)} %copy-done.28, ...), custom_call_target="tpu_custom_call" | custom-call | flops 3019898880 | bytes 13238272 | tf_op jit(solution)/shard_map/project_out/pallas_call | solution.py:262
  541.8 6.4 %collective-permute-start.65 = (bf16[2,192,640]{2,1,0:T(8,128)(2,1)S(1)}, bf16[2,192,640]{2,1,0:T(8,128)(2,1)}, u32[]{:S(2)}, u32[]{:S(2)}) collective-permute-start(bf16[2,192,640]{2,1,0:T(8,128)(2,1)S(1)} %get-tuple-element.50), channel_id=1, source_target_pairs={{0,0},{1,4},{4,1},{5,5},{8,16},{9,20},{12,17},{13,21},{16,8},{17,1... | collective-permute-start | bytes 1474568 | tf_op jit(solution)/shard_map/ppermute | solution.py:389
  548.2 6.7 %collective-permute-done.64 = bf16[2,192,640]{2,1,0:T(8,128)(2,1)S(1)} collective-permute-done((bf16[2,192,640]{2,1,0:T(8,128)(2,1)S(1)}, bf16[2,192,640]{2,1,0:T(8,128)(2,1)S(1)}, u32[]{:S(2)}, u32[]{:S(2)}) %collective-permute-start.64) | collective-permute-done | bytes 491552 | tf_op jit(solution)/shard_map/ppermute | solution.py:389
  554.8 13.8 %collective-permute-done.65 = bf16[2,192,640]{2,1,0:T(8,128)(2,1)} collective-permute-done((bf16[2,192,640]{2,1,0:T(8,128)(2,1)S(1)}, bf16[2,192,640]{2,1,0:T(8,128)(2,1)}, u32[]{:S(2)}, u32[]{:S(2)}) %collective-permute-start.65) | collective-permute-done | bytes 491552 | tf_op jit(solution)/shard_map/ppermute | solution.py:389
  (215 shorter events, 187.8 us)
Async XLA Ops:
  35.0 31.7 %collective-permute-start.4 = (bf16[192,2560]{1,0:T(8,128)(2,1)}, bf16[192,2560]{1,0:T(8,128)(2,1)S(1)}, u32[]{:S(2)}, u32[]{:S(2)}) collective-permute-start(bf16[192,2560]{1,0:T(8,128)(2,1)} %collective-permute-done), channel_id=1, source_target_pairs={{4,0},{8,4},{5,1},{9,5},{6,2},{10,6},{7,3},{11,7},{20,16},{24,20},... | collective-permute-start | bytes 2949128 | tf_op jit(solution)/shard_map/ppermute | solution.py:326
  55.4 76.7 %collective-permute-start.30 = (bf16[1536,640]{1,0:T(8,128)(2,1)}, bf16[1536,640]{1,0:T(8,128)(2,1)}, u32[]{:S(2)}, u32[]{:S(2)}) collective-permute-start(bf16[1536,640]{1,0:T(8,128)(2,1)} %bitcast.19), channel_id=1, source_target_pairs={{0,2},{2,0},{1,3},{3,1},{4,6},{6,4},{5,7},{7,5},{8,10},{10,8},{9,1... | collective-permute-start | bytes 5898248 | tf_op jit(solution)/shard_map/ppermute | solution.py:34
  62.9 27.0 %collective-permute-start.7 = (bf16[192,2560]{1,0:T(8,128)(2,1)}, bf16[192,2560]{1,0:T(8,128)(2,1)S(1)}, u32[]{:S(2)}, u32[]{:S(2)}) collective-permute-start(bf16[192,2560]{1,0:T(8,128)(2,1)} %collective-permute-done), channel_id=1, source_target_pairs={{0,1},{1,0},{4,5},{5,4},{8,9},{9,8},{2,3},{3,2},{6,7},{7,6},{10,11... | collective-permute-start | bytes 2949128 | tf_op jit(solution)/shard_map/ppermute | solution.py:329
  66.0 29.0 %collective-permute-start.10 = (bf16[192,2560]{1,0:T(8,128)(2,1)}, bf16[192,2560]{1,0:T(8,128)(2,1)S(1)}, u32[]{:S(2)}, u32[]{:S(2)}) collective-permute-start(bf16[192,2560]{1,0:T(8,128)(2,1)} %collective-permute-done.2), channel_id=1, source_target_pairs={{8,9},{9,8},{12,13},{13,12},{10,11},{11,10},{14,15},{15,14},{24,25... | collective-permute-start | bytes 2949128 | tf_op jit(solution)/shard_map/ppermute | solution.py:328
  89.9 39.5 %collective-permute-start.12 = (bf16[192,2560]{1,0:T(8,128)(2,1)S(1)}, bf16[192,2560]{1,0:T(8,128)(2,1)S(1)}, u32[]{:S(2)}, u32[]{:S(2)}) collective-permute-start(bf16[192,2560]{1,0:T(8,128)(2,1)S(1)} %collective-permute-done.1), channel_id=1, source_target_pairs={{4,5},{5,4},{8,9},{9,8},{12,13},{13,12},{6,7},{7,6},{10,11},{11,10... | collective-permute-start | bytes 2949128 | tf_op jit(solution)/shard_map/ppermute | solution.py:328
  93.1 36.4 %collective-permute-start.11 = (bf16[192,2560]{1,0:T(8,128)(2,1)S(1)}, bf16[192,2560]{1,0:T(8,128)(2,1)S(1)}, u32[]{:S(2)}, u32[]{:S(2)}) collective-permute-start(bf16[192,2560]{1,0:T(8,128)(2,1)S(1)} %collective-permute-done.5), channel_id=1, source_target_pairs={{0,1},{1,0},{2,3},{3,2},{16,17},{17,16},{18,19},{19,18}} | collective-permute-start | bytes 2949128 | tf_op jit(solution)/shard_map/ppermute | solution.py:329
  95.0 167.9 %collective-permute-start.6 = (bf16[768,2560]{1,0:T(8,128)(2,1)}, bf16[768,2560]{1,0:T(8,128)(2,1)}, u32[]{:S(2)}, u32[]{:S(2)}) collective-permute-start(bf16[768,2560]{1,0:T(8,128)(2,1)} %select_dynamic-update-slice_fusion.3.own_ref), channel_id=1, source_target_pairs={{0,16},{1,17},{2,18},{3,19},{4,20},{5,21},{6,22},{7,23},{8,24},{9,... | collective-permute-start | bytes 11796488 | tf_op jit(solution)/shard_map/ppermute | solution.py:337
  130.7 133.4 %collective-permute-start.13 = (bf16[768,2560]{1,0:T(8,128)(2,1)}, bf16[768,2560]{1,0:T(8,128)(2,1)}, u32[]{:S(2)}, u32[]{:S(2)}) collective-permute-start(bf16[768,2560]{1,0:T(8,128)(2,1)} %select_dynamic-update-slice_fusion.own_ref), channel_id=1, source_target_pairs={{0,16},{1,17},{2,18},{3,19},{4,20},{5,21},{6,22},{7,23},{8,24},{9,... | collective-permute-start | bytes 11796488 | tf_op jit(solution)/shard_map/ppermute | solution.py:337
  136.6 94.8 %collective-permute-start.31 = (bf16[1536,640]{1,0:T(8,128)(2,1)}, bf16[1536,640]{1,0:T(8,128)(2,1)}, u32[]{:S(2)}, u32[]{:S(2)}) collective-permute-start(bf16[1536,640]{1,0:T(8,128)(2,1)} %get-tuple-element.46), channel_id=1, source_target_pairs={{0,1},{1,0},{2,3},{3,2},{4,5},{5,4},{6,7},{7,6},{8,9},{9,8},{10,11... | collective-permute-start | bytes 5898248 | tf_op jit(solution)/shard_map/ppermute | solution.py:34
  167.3 49.6 %collective-permute-start.35 = (bf16[3,640,128]{2,1,0:T(8,128)(2,1)S(1)}, bf16[3,640,128]{2,1,0:T(8,128)(2,1)S(1)}, u32[]{:S(2)}, u32[]{:S(2)}) collective-permute-start(bf16[3,640,128]{2,1,0:T(8,128)(2,1)S(1)} %get-tuple-element.37), channel_id=1, source_target_pairs={{0,8},{4,12},{8,0},{12,4},{1,9},{5,13},{9,1},{13,5},{2,10},{6,14},... | collective-permute-start | bytes 1474568 | tf_op jit(solution)/shard_map/ppermute | solution.py:39
  171.4 50.2 %collective-permute-start.19 = (bf16[3,640,128]{2,1,0:T(8,128)(2,1)}, bf16[3,640,128]{2,1,0:T(8,128)(2,1)}, u32[]{:S(2)}, u32[]{:S(2)}) collective-permute-start(bf16[3,640,128]{2,1,0:T(8,128)(2,1)} %get-tuple-element.39), channel_id=1, source_target_pairs={{0,12},{4,0},{8,4},{12,8},{1,13},{5,1},{9,5},{13,9},{2,14},{6,2},{... | collective-permute-start | bytes 1474568 | tf_op jit(solution)/shard_map/ppermute | solution.py:39
  221.6 73.8 %collective-permute-start.14 = (bf16[3,640,384]{2,1,0:T(8,128)(2,1)S(1)}, bf16[3,640,384]{2,1,0:T(8,128)(2,1)S(1)}, u32[]{:S(2)}, u32[]{:S(2)}) collective-permute-start(bf16[3,640,384]{2,1,0:T(8,128)(2,1)S(1)} %dynamic-slice_bitcast_fusion), channel_id=1, source_target_pairs={{0,2},{2,0},{1,3},{3,1},{4,6},{6,4},{5,7},{7,5},{8,10},{10,8},{9,1... | collective-permute-start | bytes 4423688 | tf_op jit(solution)/shard_map/ppermute | solution.py:34
  231.5 31.2 %collective-permute-start.50 = (bf16[3,640,128]{2,1,0:T(8,128)(2,1)}, bf16[3,640,128]{2,1,0:T(8,128)(2,1)}, u32[]{:S(2)}, u32[]{:S(2)}) collective-permute-start(bf16[3,640,128]{2,1,0:T(8,128)(2,1)} %get-tuple-element.42), channel_id=1, source_target_pairs={{0,8},{4,12},{8,0},{12,4},{1,9},{5,13},{9,1},{13,5},{2,10},{6,14},... | collective-permute-start | bytes 1474568 | tf_op jit(solution)/shard_map/ppermute | solution.py:39
  243.5 189.1 %collective-permute-start.32 = (bf16[2,1536,640]{2,1,0:T(8,128)(2,1)}, bf16[2,1536,640]{2,1,0:T(8,128)(2,1)}, u32[]{:S(2)}, u32[]{:S(2)}) collective-permute-start(bf16[2,1536,640]{2,1,0:T(8,128)(2,1)} %pad_maximum_fusion.1), channel_id=1, source_target_pairs={{16,0},{17,1},{18,2},{19,3},{20,4},{21,5},{22,6},{23,7},{24,8},{25... | collective-permute-start | bytes 11796488 | tf_op jit(solution)/shard_map/ppermute | solution.py:347
  264.1 31.0 %collective-permute-start.51 = (bf16[3,640,128]{2,1,0:T(8,128)(2,1)}, bf16[3,640,128]{2,1,0:T(8,128)(2,1)}, u32[]{:S(2)}, u32[]{:S(2)}) collective-permute-start(bf16[3,640,128]{2,1,0:T(8,128)(2,1)} %collective-permute-done.50.refs_4_), channel_id=1, source_target_pairs={{0,2},{2,0},{1,3},{3,1},{4,6},{6,4},{5,7},{7,5},{8,10},{10,8},{9,1... | collective-permute-start | bytes 1474568 | tf_op jit(solution)/shard_map/ppermute | solution.py:34
  282.0 28.4 %collective-permute-start.33 = (bf16[3,640,128]{2,1,0:T(8,128)(2,1)}, bf16[3,640,128]{2,1,0:T(8,128)(2,1)}, u32[]{:S(2)}, u32[]{:S(2)}) collective-permute-start(bf16[3,640,128]{2,1,0:T(8,128)(2,1)} %get-tuple-element.38), channel_id=1, source_target_pairs={{0,4},{4,8},{8,12},{12,0},{1,5},{5,9},{9,13},{13,1},{2,6},{6,10},{... | collective-permute-start | bytes 1474568 | tf_op jit(solution)/shard_map/ppermute | solution.py:39
  285.2 26.4 %collective-permute-start.20 = (bf16[3,640,128]{2,1,0:T(8,128)(2,1)}, bf16[3,640,128]{2,1,0:T(8,128)(2,1)}, u32[]{:S(2)}, u32[]{:S(2)}) collective-permute-start(bf16[3,640,128]{2,1,0:T(8,128)(2,1)} %collective-permute-done.19.refs_6_), channel_id=1, source_target_pairs={{0,2},{2,0},{1,3},{3,1},{4,6},{6,4},{5,7},{7,5},{8,10},{10,8},{9,1... | collective-permute-start | bytes 1474568 | tf_op jit(solution)/shard_map/ppermute | solution.py:34
  295.4 31.4 %collective-permute-start.16 = (bf16[3,640,128]{2,1,0:T(8,128)(2,1)}, bf16[3,640,128]{2,1,0:T(8,128)(2,1)}, u32[]{:S(2)}, u32[]{:S(2)}) collective-permute-start(bf16[3,640,128]{2,1,0:T(8,128)(2,1)} %collective-permute-done.15.refs_2_), channel_id=1, source_target_pairs={{0,2},{2,0},{1,3},{3,1},{4,6},{6,4},{5,7},{7,5},{8,10},{10,8},{9,1... | collective-permute-start | bytes 1474568 | tf_op jit(solution)/shard_map/ppermute | solution.py:34
  310.4 30.2 %collective-permute-start.38 = (bf16[3,640,128]{2,1,0:T(8,128)(2,1)S(1)}, bf16[3,640,128]{2,1,0:T(8,128)(2,1)S(1)}, u32[]{:S(2)}, u32[]{:S(2)}) collective-permute-start(bf16[3,640,128]{2,1,0:T(8,128)(2,1)S(1)} %collective-permute-done.37.refs_6_), channel_id=1, source_target_pairs={{0,2},{2,0},{1,3},{3,1},{4,6},{6,4},{5,7},{7,5},{8,10},{10,8},{9,1... | collective-permute-start | bytes 1474568 | tf_op jit(solution)/shard_map/ppermute | solution.py:34
  311.6 36.1 %collective-permute-start.36 = (bf16[3,640,128]{2,1,0:T(8,128)(2,1)S(1)}, bf16[3,640,128]{2,1,0:T(8,128)(2,1)S(1)}, u32[]{:S(2)}, u32[]{:S(2)}) collective-permute-start(bf16[3,640,128]{2,1,0:T(8,128)(2,1)S(1)} %copy-done.18), channel_id=1, source_target_pairs={{0,2},{2,0},{1,3},{3,1},{4,6},{6,4},{5,7},{7,5},{8,10},{10,8},{9,1... | collective-permute-start | bytes 1474568 | tf_op jit(solution)/shard_map/ppermute | solution.py:34
  316.2 42.0 %collective-permute-start.34 = (bf16[3,640,128]{2,1,0:T(8,128)(2,1)}, bf16[3,640,128]{2,1,0:T(8,128)(2,1)S(1)}, u32[]{:S(2)}, u32[]{:S(2)}) collective-permute-start(bf16[3,640,128]{2,1,0:T(8,128)(2,1)} %collective-permute-done.33.refs_2_), channel_id=1, source_target_pairs={{0,2},{2,0},{1,3},{3,1},{4,6},{6,4},{5,7},{7,5},{8,10},{10,8},{9,1... | collective-permute-start | bytes 1474568 | tf_op jit(solution)/shard_map/ppermute | solution.py:34
  326.7 48.3 %collective-permute-start.54 = (bf16[2,768,256]{2,1,0:T(8,128)(2,1)}, bf16[2,768,256]{2,1,0:T(8,128)(2,1)S(1)}, u32[]{:S(2)}, u32[]{:S(2)}) collective-permute-start(bf16[2,768,256]{2,1,0:T(8,128)(2,1)} %get-tuple-element.27.own_ref), channel_id=1, source_target_pairs={{0,2},{2,0},{1,3},{3,1},{4,6},{6,4},{5,7},{7,5},{8,10},{10,8},{9,1... | collective-permute-start | bytes 2359304 | tf_op jit(solution)/shard_map/ppermute | solution.py:34
  340.6 51.5 %collective-permute-start.21 = (bf16[2,768,256]{2,1,0:T(8,128)(2,1)}, bf16[2,768,256]{2,1,0:T(8,128)(2,1)}, u32[]{:S(2)}, u32[]{:S(2)}) collective-permute-start(bf16[2,768,256]{2,1,0:T(8,128)(2,1)} %get-tuple-element.19.own_ref), channel_id=1, source_target_pairs={{0,2},{2,0},{1,3},{3,1},{4,6},{6,4},{5,7},{7,5},{8,10},{10,8},{9,1... | collective-permute-start | bytes 2359304 | tf_op jit(solution)/shard_map/ppermute | solution.py:34
  372.6 36.3 %collective-permute-start.39 = (bf16[2,768,256]{2,1,0:T(8,128)(2,1)}, bf16[2,768,256]{2,1,0:T(8,128)(2,1)}, u32[]{:S(2)}, u32[]{:S(2)}) collective-permute-start(bf16[2,768,256]{2,1,0:T(8,128)(2,1)} %get-tuple-element.23.own_ref), channel_id=1, source_target_pairs={{0,2},{2,0},{1,3},{3,1},{4,6},{6,4},{5,7},{7,5},{8,10},{10,8},{9,1... | collective-permute-start | bytes 2359304 | tf_op jit(solution)/shard_map/ppermute | solution.py:34
  383.7 37.3 %collective-permute-start.55 = (bf16[384,128]{1,0:T(8,128)(2,1)}, bf16[384,128]{1,0:T(8,128)(2,1)S(1)}, u32[]{:S(2)}, u32[]{:S(2)}) collective-permute-start(bf16[384,128]{1,0:T(8,128)(2,1)} %get-tuple-element.29), channel_id=1, source_target_pairs={{16,0},{17,1},{18,2},{19,3},{20,4},{21,5},{22,6},{23,7},{24,8},{25... | collective-permute-start | bytes 294920 | tf_op jit(solution)/shard_map/ppermute | solution.py:359
  399.9 28.3 %collective-permute-start.22 = (bf16[384,128]{1,0:T(8,128)(2,1)}, bf16[384,128]{1,0:T(8,128)(2,1)S(1)}, u32[]{:S(2)}, u32[]{:S(2)}) collective-permute-start(bf16[384,128]{1,0:T(8,128)(2,1)} %get-tuple-element.21), channel_id=1, source_target_pairs={{16,0},{17,1},{18,2},{19,3},{20,4},{21,5},{22,6},{23,7},{24,8},{25... | collective-permute-start | bytes 294920 | tf_op jit(solution)/shard_map/ppermute | solution.py:359
  476.0 48.5 %collective-permute-start.26 = (bf16[1152,128]{1,0:T(8,128)(2,1)S(1)}, bf16[1152,128]{1,0:T(8,128)(2,1)S(1)}, u32[]{:S(2)}, u32[]{:S(2)}) collective-permute-start(bf16[1152,128]{1,0:T(8,128)(2,1)S(1)} %select_dynamic-update-slice_fusion.8.refs_0_), channel_id=1, source_target_pairs={{0,1},{1,0},{2,3},{3,2},{4,5},{5,4},{6,7},{7,6},{8,9},{9,8},{10,11... | collective-permute-start | bytes 884744 | tf_op jit(solution)/shard_map/ppermute | solution.py:34
  486.4 38.2 %collective-permute-start.27 = (bf16[1152,128]{1,0:T(8,128)(2,1)S(1)}, bf16[1152,128]{1,0:T(8,128)(2,1)S(1)}, u32[]{:S(2)}, u32[]{:S(2)}) collective-permute-start(bf16[1152,128]{1,0:T(8,128)(2,1)S(1)} %collective-permute-done.23.refs_1_), channel_id=1, source_target_pairs={{0,1},{1,0},{2,3},{3,2},{4,5},{5,4},{6,7},{7,6},{8,9},{9,8},{10,11... | collective-permute-start | bytes 884744 | tf_op jit(solution)/shard_map/ppermute | solution.py:34
  486.5 38.1 %collective-permute-start.28 = (bf16[1152,128]{1,0:T(8,128)(2,1)S(1)}, bf16[1152,128]{1,0:T(8,128)(2,1)S(1)}, u32[]{:S(2)}, u32[]{:S(2)}) collective-permute-start(bf16[1152,128]{1,0:T(8,128)(2,1)S(1)} %collective-permute-done.24.refs_2_), channel_id=1, source_target_pairs={{0,1},{1,0},{2,3},{3,2},{4,5},{5,4},{6,7},{7,6},{8,9},{9,8},{10,11... | collective-permute-start | bytes 884744 | tf_op jit(solution)/shard_map/ppermute | solution.py:34
  488.0 36.7 %collective-permute-start.29 = (bf16[1152,128]{1,0:T(8,128)(2,1)S(1)}, bf16[1152,128]{1,0:T(8,128)(2,1)S(1)}, u32[]{:S(2)}, u32[]{:S(2)}) collective-permute-start(bf16[1152,128]{1,0:T(8,128)(2,1)S(1)} %collective-permute-done.25.refs_3_), channel_id=1, source_target_pairs={{0,1},{1,0},{2,3},{3,2},{4,5},{5,4},{6,7},{7,6},{8,9},{9,8},{10,11... | collective-permute-start | bytes 884744 | tf_op jit(solution)/shard_map/ppermute | solution.py:34
  488.1 26.3 %collective-permute-start.47 = (bf16[1152,128]{1,0:T(8,128)(2,1)S(1)}, bf16[1152,128]{1,0:T(8,128)(2,1)S(1)}, u32[]{:S(2)}, u32[]{:S(2)}) collective-permute-start(bf16[1152,128]{1,0:T(8,128)(2,1)S(1)} %collective-permute-done.43.refs_3_), channel_id=1, source_target_pairs={{0,1},{1,0},{2,3},{3,2},{4,5},{5,4},{6,7},{7,6},{8,9},{9,8},{10,11... | collective-permute-start | bytes 884744 | tf_op jit(solution)/shard_map/ppermute | solution.py:34
  541.8 26.8 %collective-permute-start.65 = (bf16[2,192,640]{2,1,0:T(8,128)(2,1)S(1)}, bf16[2,192,640]{2,1,0:T(8,128)(2,1)}, u32[]{:S(2)}, u32[]{:S(2)}) collective-permute-start(bf16[2,192,640]{2,1,0:T(8,128)(2,1)S(1)} %get-tuple-element.50), channel_id=1, source_target_pairs={{0,0},{1,4},{4,1},{5,5},{8,16},{9,20},{12,17},{13,21},{16,8},{17,1... | collective-permute-start | bytes 1474568 | tf_op jit(solution)/shard_map/ppermute | solution.py:389
  (69 other events, 1304.9 us)
where the time goes:
time: 574 us; the launch traced here: 573 us
  waiting for transfers between devices  315 us (55%)
  Pallas kernels  104 us (18%)
  starting transfers between devices  103 us (18%)
  other arithmetic  31.6 us (6%)
  local copies, waits for them, and re-layouts  17.9 us (3%)
    ppermute x18, waiting for transfers between devices, shift(): lax.ppermute(x, axis, [(i, (i + distance) % size) for i in range(size)])  145 us
    ppermute x28, waiting for transfers between devices, swap(): return lax.ppermute(x, axis, [(0, 1), (1, 0)])  67.3 us
    pallas_call x3, Pallas kernels, project(): pl.pallas_call(project_kernel, name='project', grid_spec=pltpu.PrefetchSc...  41 us
    ppermute x3, waiting for transfers between devices, split_step(): lax.ppermute(ups[-1][0], 'outer', [(i, i + 1) for i in range(k - 1, nz -...  36.3 us
    ppermute x18, starting transfers between devices, shift(): lax.ppermute(x, axis, [(i, (i + distance) % size) for i in range(size)])  25.1 us
    pallas_call x3, Pallas kernels, attend(): pl.pallas_call(attend_kernel, name='attend', grid_spec=pltpu.PrefetchScal...  23.4 us
    ppermute x2, waiting for transfers between devices, split_step(): received.append(lax.ppermute(block, axes, pairs))  20.4 us
    ppermute x3, waiting for transfers between devices, split_step(): ups = ups + [(up, lax.ppermute(up, ('outer', 'fsdp'), pairs[k * nf:]))]  19.9 us
  transfers between devices with their start and end apart: 66, of which 30 were waited for; matrix products, arithmetic and copies ran while one was open for 7% of the time, Pallas kernels for 17%

commit v1 on v0

--- a/solution.py
+++ b/solution.py
@@ -78,114 +78,127 @@
     )(b, order, time_index, latents, noise)
 
 
+def gather_kernel(b_ref, at_ref, cfg_ref, z_ref, *refs):
+    own_ref, *pieces, gain_ref, table_ref, x_ref, o_ref = refs
+    tok = own_ref.shape[0]
+    count = len(pieces) // 2 + 1
+    z = z_ref[0]
+    gain_row = gain_ref[...]
+    shift_row = table_ref[pl.ds(cfg_ref[1 - b_ref[0]], 1), :]
+    for k in range(count):
+        if k == 0:
+            rows = own_ref[...]
+        else:
+            rows = jnp.where(z + k < count, pieces[2 * k - 2][...], pieces[2 * k - 1][...])
+        to = pl.ds(pl.multiple_of((z + k) % count * tok, tok), tok)
+        x_ref[to, :] = rows
+        o_ref[to, :] = (rows.astype(jnp.float32) * gain_row + shift_row).astype(jnp.bfloat16)
+
+
 def affine_kernel(b_ref, at_ref, cfg_ref, own_ref, main_ref, gain_ref, table_ref, o_ref):
-    b = b_ref[0]
-    gain_row = gain_ref[...]
-    own = own_ref[...]
-    main = jnp.where(b == 0, own, main_ref[...]).astype(jnp.float32)
+    main = jnp.where(b_ref[0] == 0, own_ref[...], main_ref[...]).astype(jnp.float32)
     cond = table_ref[pl.ds(cfg_ref[0], 1), :]
-    second = table_ref[pl.ds(cfg_ref[1 - b], 1), :]
-    o_ref[0] = (main * gain_row + cond).astype(jnp.bfloat16)
-    o_ref[1] = (own.astype(jnp.float32) * gain_row + second).astype(jnp.bfloat16)
-
-
-def affine(b, order, cfg_pair, own_rows, main_rows, gain, table):
-    rows, width = own_rows.shape
-    blocks = order.shape[0]
-    size = width // blocks
-    table = table.astype(jnp.float32)
-    block = pl.BlockSpec((rows, size), lambda p, *_: (0, p))
+    o_ref[...] = (main * gain_ref[...] + cond).astype(jnp.bfloat16)
+
+
+def columns(kernel, scalars, arrays, gain, table, rows, outputs):
+    order = scalars[1]
+    width = arrays[0].shape[1]
+    size = width // order.shape[0]
+
+    def block(height):
+        return pl.BlockSpec((height, size), lambda p, *_: (0, p))
+
+    def turned(height):
+        return pl.BlockSpec((height, size), lambda p, b, at, *_: (0, at[p]))
+
     return pl.pallas_call(
-        affine_kernel,
-        name="affine",
+        kernel,
         grid_spec=pltpu.PrefetchScalarGridSpec(
-            num_scalar_prefetch=3,
-            grid=(blocks,),
-            in_specs=[
-                block,
-                block,
-                pl.BlockSpec((1, size), lambda p, b, at, cfg: (0, at[p])),
-                pl.BlockSpec((table.shape[0], size), lambda p, b, at, cfg: (0, at[p])),
-            ],
-            out_specs=pl.BlockSpec((2, rows, size), lambda p, *_: (0, 0, p)),
-        ),
-        out_shape=jax.ShapeDtypeStruct((2, rows, width), jnp.bfloat16),
+            num_scalar_prefetch=len(scalars),
+            grid=(order.shape[0],),
+            in_specs=[block(a.shape[0]) for a in arrays] + [turned(1), turned(table.shape[0])],
+            out_specs=[block(rows)] * outputs,
+        ),
+        out_shape=[jax.ShapeDtypeStruct((rows, width), jnp.bfloat16)] * outputs,
         cost_estimate=pl.CostEstimate(
-            flops=4 * rows * width, transcendentals=0, bytes_accessed=8 * rows * width
-        ),
-    )(b, order, cfg_pair, own_rows, main_rows, gain, table)
-
-
-def project_kernel(place_ref, mine_ref, theirs_ref, *refs):
-    blocks, (q_ref, kv_ref) = refs[:-2], refs[-2:]
-    total = None
+            flops=2 * rows * width, transcendentals=0, bytes_accessed=6 * rows * width
+        ),
+    )(*scalars, *arrays, gain, table)
+
+
+def project_kernel(place_ref, *refs):
+    inputs, blocks, (q_ref, kv_ref) = refs[:4], refs[4:-2], refs[-2:]
+    totals = [None, None]
     for d in range(len(blocks) // 2):
         pair = blocks[2 * d : 2 * d + 2]
         weight = jnp.concatenate(
             [jnp.concatenate([w[j] for j in range(3)], axis=1) for w in pair], axis=0
         )
         depth = weight.shape[0]
-        each = mine_ref.shape[2] // depth
+        each = inputs[0].shape[1] // depth
         here = pl.ds(pl.multiple_of(place_ref[d] % each * depth, HD), depth)
-        rows = jnp.where(place_ref[d] < each, mine_ref[0, :, here], theirs_ref[0, :, here])
-        part = jnp.dot(rows, weight, preferred_element_type=jnp.float32)
-        total = part if total is None else total + part
-    total = total.astype(jnp.bfloat16)
-    q_ref[0] = total[:, :HD]
-    kv_ref[0] = total[:, HD:]
-
-
-def project(mine, theirs, places, weights, own_swapped, pieces, head):
-    passes, rows, half = mine.shape
+        for p in range(2):
+            mine, theirs = inputs[2 * p : 2 * p + 2]
+            rows = jnp.where(place_ref[d] < each, mine[:, here], theirs[:, here])
+            part = jnp.dot(rows, weight, preferred_element_type=jnp.float32)
+            totals[p] = part if d == 0 else totals[p] + part
+    for p in range(2):
+        total = totals[p].astype(jnp.bfloat16)
+        q_ref[p] = total[:, :HD]
+        kv_ref[p] = total[:, HD:]
+
+
+def project(inputs, places, weights, own_swapped, pieces, head):
+    rows, half = inputs[0].shape
     width = 2 * half
     depth = weights.shape[1]
-    tile = rows // 2 if rows % 32 == 0 else rows
-    whole = pl.BlockSpec((3, depth, HD), lambda p, t, at: (0, 0, 0))
+    tile = rows // 4 if rows % 64 == 0 else rows
+    whole = pl.BlockSpec((3, depth, HD), lambda t, at: (0, 0, 0))
     return pl.pallas_call(
         project_kernel,
         name="project",
         grid_spec=pltpu.PrefetchScalarGridSpec(
             num_scalar_prefetch=1,
-            grid=(passes, rows // tile),
-            in_specs=[
-                pl.BlockSpec((1, tile, half), lambda p, t, at: (p, t, 0)),
-                pl.BlockSpec((1, tile, half), lambda p, t, at: (p, t, 0)),
-                pl.BlockSpec((3, depth, HD), lambda p, t, at: (0, 0, at[at.shape[0] - 1] + head)),
-                pl.BlockSpec((3, depth, HD), lambda p, t, at: (0, 0, head)),
+            grid=(rows // tile,),
+            in_specs=[pl.BlockSpec((tile, half), lambda t, at: (t, 0))] * 4
+            + [
+                pl.BlockSpec((3, depth, HD), lambda t, at: (0, 0, at[at.shape[0] - 1] + head)),
+                pl.BlockSpec((3, depth, HD), lambda t, at: (0, 0, head)),
             ]
             + [whole] * len(pieces),
             out_specs=[
-                pl.BlockSpec((1, tile, HD), lambda p, t, at: (p, t, 0)),
-                pl.BlockSpec((1, tile, 2 * HD), lambda p, t, at: (p, t, 0)),
+                pl.BlockSpec((2, tile, HD), lambda t, at: (0, t, 0)),
+                pl.BlockSpec((2, tile, 2 * HD), lambda t, at: (0, t, 0)),
             ],
         ),
         out_shape=[
-            jax.ShapeDtypeStruct((passes, rows, HD), jnp.bfloat16),
-            jax.ShapeDtypeStruct((passes, rows, 2 * HD), jnp.bfloat16),
+            jax.ShapeDtypeStruct((2, rows, HD), jnp.bfloat16),
+            jax.ShapeDtypeStruct((2, rows, 2 * HD), jnp.bfloat16),
         ],
         cost_estimate=pl.CostEstimate(
-            flops=6 * passes * rows * width * HD,
+            flops=12 * rows * width * HD,
             transcendentals=0,
-            bytes_accessed=2 * (passes * rows * (width + 3 * HD) + 3 * width * HD),
-        ),
-    )(places, mine, theirs, weights, own_swapped, *pieces)
+            bytes_accessed=2 * (2 * rows * (width + 3 * HD) + 3 * width * HD),
+        ),
+    )(places, *inputs, weights, own_swapped, *pieces)
 
 
 def attend_kernel(b_ref, q_ref, own_ref, other_ref, o_ref, give_ref):
     dims = (((1,), (1,)), ((), ()))
-    scale = HD ** (-0.5)
+    scale = HD ** (-0.5) * math.log2(math.e)
     tile = q_ref.shape[1]
     step, steps = pl.program_id(0), pl.num_programs(0)
     mixed = []
     for p in range(2):
         q, own, other = q_ref[p], own_ref[p], other_ref[p]
-        s0 = lax.dot_general(q, own[:, :HD], dims, preferred_element_type=jnp.float32) * scale
-        s1 = lax.dot_general(q, other[:, :HD], dims, preferred_element_type=jnp.float32) * scale
+        s0 = lax.dot_general(q, own[:, :HD], dims, preferred_element_type=jnp.float32)
+        s1 = lax.dot_general(q, other[:, :HD], dims, preferred_element_type=jnp.float32)
         peak = jnp.maximum(
             jnp.max(s0, axis=1, keepdims=True), jnp.max(s1, axis=1, keepdims=True)
         )
-        p0 = jnp.exp(s0 - peak)
-        p1 = jnp.exp(s1 - peak)
+        p0 = jnp.exp2((s0 - peak) * scale)
+        p1 = jnp.exp2((s1 - peak) * scale)
         mass = jnp.sum(p0, axis=1, keepdims=True) + jnp.sum(p1, axis=1, keepdims=True)
         total = jnp.dot(p0.astype(jnp.bfloat16), own[:, HD:], preferred_element_type=jnp.float32)
         total += jnp.dot(
@@ -239,36 +252,41 @@
     )(b, q, own, other)
 
 
-def project_out_kernel(count, first, at_ref, *refs):
-    pieces, weights, refs = refs[:count], refs[count : 2 * count], refs[2 * count :]
+def project_out_kernel(count, choices, first, at_ref, *refs):
+    pieces, weights = refs[:count], refs[count : (1 + choices) * count]
     rows = jnp.concatenate([a[...] for a in pieces], axis=1)
-    weight = jnp.concatenate([w[0] for w in weights], axis=0)
+    weight = jnp.concatenate([w[...] for w in weights[:count]], axis=0)
+    if choices == 2:
+        other = jnp.concatenate([w[...] for w in weights[count:]], axis=0)
+        weight = jnp.where(at_ref[at_ref.shape[0] - 1] == 0, weight, other)
     total = jnp.dot(rows, weight, preferred_element_type=jnp.float32)
-    refs[-1][...] = total if first else refs[0][...] + total
-
-
-def project_out(sets, tiles, places, mine, theirs, carry):
+    refs[-1][...] = total if first else refs[-2][...] + total
+
+
+def project_out(sets, tiles, places, choices, carry):
     tile = sets[0][1][0].shape[0] // 3
     each = len(sets[0][1]) // 2
     count = 2 * each * len(sets)
-    width = mine.shape[2]
+    width = choices[0][0].shape[1]
     lo, hi = tiles
     rows = (hi - lo) * tile
     first = carry is None
 
     def weight_spec(k, head):
-        return pl.BlockSpec((1, HD, width), lambda t, at: ((t + lo) // 2, at[k] + head, 0))
-
+        return pl.BlockSpec((HD, width), lambda t, at: (at[k] + head, 0))
+
+    weight_specs = [weight_spec(k % each, head) for head, _ in sets for k in range(2 * each)]
+    o_spec = pl.BlockSpec((tile, width), lambda t, at: (t, 0))
     return pl.pallas_call(
-        functools.partial(project_out_kernel, count, first),
+        functools.partial(project_out_kernel, count, len(choices), first),
         name="project_out",
         grid_spec=pltpu.PrefetchScalarGridSpec(
             num_scalar_prefetch=1,
             grid=(hi - lo,),
             in_specs=[pl.BlockSpec((tile, HD), lambda t, at: (t + lo, 0))] * count
-            + [weight_spec(k % each, head) for head, _ in sets for k in range(2 * each)]
-            + ([] if first else [pl.BlockSpec((tile, width), lambda t, at: (t + lo, 0))]),
-            out_specs=pl.BlockSpec((tile, width), lambda t, at: (t, 0)),
+            + weight_specs * len(choices)
+            + ([] if first else [o_spec]),
+            out_specs=o_spec,
         ),
         out_shape=jax.ShapeDtypeStruct((rows, width), jnp.float32),
         cost_estimate=pl.CostEstimate(
@@ -279,7 +297,7 @@
     )(
         places,
         *[piece for _, pieces in sets for piece in pieces],
-        *(([mine] * each + [theirs] * each) * len(sets)),
+        *[w for m, t in choices for w in ([m] * each + [t] * each) * len(sets)],
         *([] if first else [carry]),
     )
 
@@ -295,8 +313,7 @@
     f = lax.axis_index("fsdp")
     nz = lax.axis_size("outer")
     nf = lax.axis_size("fsdp")
-    tok, width = latents.shape
-    half = width // nf
+    tok, _ = latents.shape
     weights = w_qkv[0]
     _, cols = weights.shape[1:]
     head_count = cols // HD // nz
@@ -327,46 +344,50 @@
         pairs = [(i * nf + j, i * nf + 1 - j) for i in range(nz) for j in range(nf)]
         ups = ups + [(up, lax.ppermute(up, ("outer", "fsdp"), pairs[k * nf :]))]
         downs = downs + [(down, lax.ppermute(down, ("outer", "fsdp"), pairs[: -k * nf]))]
-    inputs = []
+    rows = nz * tok
+    mains, seconds = [], []
     for side in range(2):
-        own_rows = jnp.zeros((nz * tok, half), jnp.bfloat16)
-        own_rows = lax.dynamic_update_slice(own_rows, unit[side], (z * tok, 0))
+        part = order[side * nz : (side + 1) * nz]
+        pieces = [unit[side]]
         for k in range(1, nz):
-            block = jnp.where(z + k < nz, downs[k][side], ups[nz - k][side])
-            own_rows = lax.dynamic_update_slice(own_rows, block, ((z + k) % nz * tok, 0))
+            pieces += [downs[k][side], ups[nz - k][side]]
+        scalars = (which, part, cfg_pair)
+        own_rows, second = columns(
+            gather_kernel, (*scalars, z[None].astype(jnp.int32)), pieces, gain, cond_table, rows, 2
+        )
         main_rows = lax.ppermute(own_rows, "branch", [(0, 1)])
-        part = order[side * nz : (side + 1) * nz]
-        inputs.append(affine(which, part, cfg_pair, own_rows, main_rows, gain, cond_table))
+        (main,) = columns(affine_kernel, scalars, [own_rows, main_rows], gain, cond_table, rows, 1)
+        mains.append(main)
+        seconds.append(second)
+    inputs = (*mains, *seconds)
 
     out_here = w_out[0]
     out_width = out_here.shape[1]
     out_there = swap(out_here, "inner")
     out_mine = jnp.where(f == y, out_here, out_there)
-    out_theirs = swap(jnp.where(f == y, out_there, out_here), "fsdp")
-    out_own = jnp.stack([out_mine, out_theirs])
-    out_critic = lax.ppermute(out_own, "branch", [(1, 0)])
-    out_critic = jnp.where(b == 0, out_critic, out_own)
-    out_pairs = jnp.stack([out_own, out_critic], axis=1)
-    out_mine, out_theirs = out_pairs[0], out_pairs[1]
-    out_places = (from_z * head_count).astype(jnp.int32)
-
-    rows = nz * tok
+    out_sent = jnp.where(f == y, out_there, out_here)
+    out_theirs = swap(out_sent, "fsdp")
+    out_own = (out_mine, out_theirs)
+    out_critic = tuple(lax.ppermute(w, "branch", [(1, 0)]) for w in out_own)
+    out_places = jnp.concatenate([from_z * head_count, b[None]]).astype(jnp.int32)
+
     sets = []
     for head in range(head_count):
-        q, pair = project(*inputs, places, weights, own_swapped, head_pieces[head], head)
+        q, pair = project(inputs, places, weights, own_swapped, head_pieces[head], head)
         other = swap(pair, "inner")
         attn, give = attend(which, q, pair, other)
         taken = lax.ppermute(give, "branch", [(1, 0)])
         attn = lax.dynamic_update_slice(attn, jnp.where(b == 0, taken, attn[rows:]), (rows, 0))
         ours, across = [attn], [swap(attn, "fsdp")]
-        for _ in range(1, nz):
-            ours.append(shift(ours[-1], "outer", 1))
+        for k in range(1, nz):
+            ours.append(shift(attn, "outer", k))
             across.append(swap(ours[-1], "fsdp"))
         sets.append((head, ours + across))
-    last = (out_places, out_mine, out_theirs)
-    early = project_out(sets[:-1], (0, 3), *last, None)
-    pred = project_out(sets[-1:], (0, 2), *last, early)
-    own_pred = project_out(sets[-1:], (2, 3), *last, early)
+    main_only, either = (out_own,), (out_critic, out_own)
+    early = project_out(sets[:-1], (0, 2), out_places, main_only, None)
+    early_own = project_out(sets[:-1], (2, 3), out_places, either, None)
+    pred = project_out(sets[-1:], (0, 2), out_places, main_only, early)
+    own_pred = project_out(sets[-1:], (2, 3), out_places, either, early_own)
 
     kept = lax.dynamic_slice_in_dim(pred, b * (rows // 2), rows // 2, 0)
     given = lax.dynamic_slice_in_dim(pred, (1 - b) * (rows // 2), rows // 2, 0)

time: 574 us -> 563 us (0.981)
  the two profiles are of different devices: /device:TPU:9 before, /device:TPU:22 now
where the time goes in v1:
time: 563 us; the launch traced here: 562 us
  waiting for transfers between devices  291 us (52%)
  starting transfers between devices  123 us (22%)
  Pallas kernels  121 us (21%)
  local copies, waits for them, and re-layouts  13.7 us (2%)
  other arithmetic  11.8 us (2%)
    ppermute x18, waiting for transfers between devices, shift(): lax.ppermute(x, axis, [(i, (i + distance) % size) for i in range(size)])  113 us
    ppermute x28, waiting for transfers between devices, swap(): return lax.ppermute(x, axis, [(0, 1), (1, 0)])  99.5 us
    ppermute x18, starting transfers between devices, shift(): lax.ppermute(x, axis, [(i, (i + distance) % size) for i in range(size)])  47.4 us
    ppermute x3, waiting for transfers between devices, split_step(): lax.ppermute(ups[-1][0], 'outer', [(i, i + 1) for i in range(k - 1, nz -...  44.1 us
    pallas_call x3, Pallas kernels, project(): pl.pallas_call(project_kernel, name='project', grid_spec=pltpu.PrefetchSc...  42.4 us
    pallas_call x4, Pallas kernels, columns(): pl.pallas_call(kernel, grid_spec=pltpu.PrefetchScalarGridSpec(num_scalar_...  28.7 us
    pallas_call x4, Pallas kernels, project_out(): pl.pallas_call(functools.partial(project_out_kernel, count, len(choices),...  23.3 us
    pallas_call x3, Pallas kernels, attend(): pl.pallas_call(attend_kernel, name='attend', grid_spec=pltpu.PrefetchScal...  22 us
  transfers between devices with their start and end apart: 67, of which 36 were waited for; matrix products, arithmetic and copies ran while one was open for 3% of the time, Pallas kernels for 21%

profile of v1, /device:TPU:22, one launch (start us, length us, event | category | flops | bytes accessed | tf_op | source)
XLA Modules:
  0.0 561.6 jit_solution(7633095974480311765)
XLA Ops:
  11.8 19.7 %collective-permute-done.1.refs_6_ = bf16[192,2560]{1,0:T(8,128)(2,1)S(1)} collective-permute-done((bf16[192,2560]{1,0:T(8,128)(2,1)}, bf16[192,2560]{1,0:T(8,128)(2,1)S(1)}, u32[]{:S(2)}, u32[]{:S(2)}) %collective-permute-start.1) | collective-permute-done | bytes 983072 | tf_op jit(solution)/shard_map/ppermute | solution.py:342
  40.8 15.2 %collective-permute-done.2.refs_4_ = bf16[192,2560]{1,0:T(8,128)(2,1)S(1)} collective-permute-done((bf16[192,2560]{1,0:T(8,128)(2,1)S(1)}, bf16[192,2560]{1,0:T(8,128)(2,1)S(1)}, u32[]{:S(2)}, u32[]{:S(2)}) %collective-permute-start.2) | collective-permute-done | bytes 983072 | tf_op jit(solution)/shard_map/ppermute | solution.py:342
  69.6 9.2 %collective-permute-done.3.refs_2_ = bf16[192,2560]{1,0:T(8,128)(2,1)} collective-permute-done((bf16[192,2560]{1,0:T(8,128)(2,1)S(1)}, bf16[192,2560]{1,0:T(8,128)(2,1)}, u32[]{:S(2)}, u32[]{:S(2)}) %collective-permute-start.3) | collective-permute-done | bytes 983072 | tf_op jit(solution)/shard_map/ppermute | solution.py:342
  83.3 7.6 %shard_map.95 = (bf16[768,2560]{1,0:T(8,128)(2,1)}, bf16[768,2560]{1,0:T(8,128)(2,1)}) custom-call(s32[1]{0:T(128)} %bitcast.4.b_ref, s32[4]{0:T(128)} %pad_add_fusion.3.at_ref, s32[2]{0:T(128)} %cfg_ref.7, s32[1]{0:T(128)} %bitcast.10.z_ref, bf16[192,2560]{1,0:T(8,128)(2,1)} %get-tuple-element.20.refs_0_, bf16[192,2560]{1,0:T(8,128)(2,1)} %copy-done.21, ...), custom_call_target="tpu_custom_call" | custom-call | flops 3932160 | bytes 11796480 | tf_op jit(solution)/shard_map/pallas_call | solution.py:115
  94.1 12.6 %collective-permute-done.10.refs_4_ = bf16[192,2560]{1,0:T(8,128)(2,1)} collective-permute-done((bf16[192,2560]{1,0:T(8,128)(2,1)S(1)}, bf16[192,2560]{1,0:T(8,128)(2,1)}, u32[]{:S(2)}, u32[]{:S(2)}) %collective-permute-start.10) | collective-permute-done | bytes 983072 | tf_op jit(solution)/shard_map/ppermute | solution.py:345
  106.7 7.7 %shard_map.97 = (bf16[768,2560]{1,0:T(8,128)(2,1)}, bf16[768,2560]{1,0:T(8,128)(2,1)}) custom-call(s32[1]{0:T(128)} %bitcast.4.b_ref, s32[4]{0:T(128)} %pad_add_fusion.4.at_ref, s32[2]{0:T(128)} %cfg_ref.7, s32[1]{0:T(128)} %bitcast.10.z_ref, bf16[192,2560]{1,0:T(8,128)(2,1)} %get-tuple-element.22.refs_0_, bf16[192,2560]{1,0:T(8,128)(2,1)} %copy-done.18, ...), custom_call_target="tpu_custom_call" | custom-call | flops 3932160 | bytes 11796480 | tf_op jit(solution)/shard_map/pallas_call | solution.py:115
  121.5 19.8 %collective-permute-start.15 = (bf16[3,640,128]{2,1,0:T(8,128)(2,1)S(1)}, bf16[3,640,128]{2,1,0:T(8,128)(2,1)}, u32[]{:S(2)}, u32[]{:S(2)}) collective-permute-start(bf16[3,640,128]{2,1,0:T(8,128)(2,1)S(1)} %get-tuple-element.47), channel_id=1, source_target_pairs={{0,4},{4,8},{8,12},{12,0},{1,5},{5,9},{9,13},{13,1},{2,6},{6,10},{... | collective-permute-start | bytes 1474568 | tf_op jit(solution)/shard_map/ppermute | solution.py:39
  141.8 7.8 %collective-permute-done.15.refs_6_ = bf16[3,640,128]{2,1,0:T(8,128)(2,1)} collective-permute-done((bf16[3,640,128]{2,1,0:T(8,128)(2,1)S(1)}, bf16[3,640,128]{2,1,0:T(8,128)(2,1)}, u32[]{:S(2)}, u32[]{:S(2)}) %collective-permute-start.15) | collective-permute-done | bytes 491552 | tf_op jit(solution)/shard_map/ppermute | solution.py:39
  149.6 18.7 %collective-permute-done.17.refs_8_ = bf16[3,640,128]{2,1,0:T(8,128)(2,1)} collective-permute-done((bf16[3,640,128]{2,1,0:T(8,128)(2,1)S(1)}, bf16[3,640,128]{2,1,0:T(8,128)(2,1)}, u32[]{:S(2)}, u32[]{:S(2)}) %collective-permute-start.17) | collective-permute-done | bytes 491552 | tf_op jit(solution)/shard_map/ppermute | solution.py:39
  172.3 17.0 %collective-permute-done.19.refs_10_ = bf16[3,640,128]{2,1,0:T(8,128)(2,1)} collective-permute-done((bf16[3,640,128]{2,1,0:T(8,128)(2,1)S(1)}, bf16[3,640,128]{2,1,0:T(8,128)(2,1)}, u32[]{:S(2)}, u32[]{:S(2)}) %collective-permute-start.19) | collective-permute-done | bytes 491552 | tf_op jit(solution)/shard_map/ppermute | solution.py:39
  192.5 18.7 %collective-permute-done.34.refs_8_ = bf16[3,640,128]{2,1,0:T(8,128)(2,1)} collective-permute-done((bf16[3,640,128]{2,1,0:T(8,128)(2,1)}, bf16[3,640,128]{2,1,0:T(8,128)(2,1)}, u32[]{:S(2)}, u32[]{:S(2)}) %collective-permute-start.34) | collective-permute-done | bytes 491552 | tf_op jit(solution)/shard_map/ppermute | solution.py:39
  214.4 12.9 %collective-permute-done.36.refs_10_ = bf16[3,640,128]{2,1,0:T(8,128)(2,1)} collective-permute-done((bf16[3,640,128]{2,1,0:T(8,128)(2,1)}, bf16[3,640,128]{2,1,0:T(8,128)(2,1)}, u32[]{:S(2)}, u32[]{:S(2)}) %collective-permute-start.36) | collective-permute-done | bytes 491552 | tf_op jit(solution)/shard_map/ppermute | solution.py:39
  237.3 6.7 %shard_map.96.refs_0_ = bf16[768,2560]{1,0:T(8,128)(2,1)} custom-call(s32[1]{0:T(128)} %bitcast.4.b_ref, s32[4]{0:T(128)} %pad_add_fusion.3.at_ref, s32[2]{0:T(128)} %cfg_ref.7, bf16[768,2560]{1,0:T(8,128)(2,1)} %get-tuple-element.21.own_ref, bf16[768,2560]{1,0:T(8,128)(2,1)} %collective-permute-done.6.main_ref, f32[1,5120]{1,0:T(1,128)} %gain_ref.3, ...), custom_call_target="tpu_custom_call" | custom-call | flops 3932160 | bytes 11796480 | tf_op jit(solution)/shard_map/pallas_call | solution.py:115
  244.0 6.7 %shard_map.98.refs_1_ = bf16[768,2560]{1,0:T(8,128)(2,1)} custom-call(s32[1]{0:T(128)} %bitcast.4.b_ref, s32[4]{0:T(128)} %pad_add_fusion.4.at_ref, s32[2]{0:T(128)} %cfg_ref.7, bf16[768,2560]{1,0:T(8,128)(2,1)} %get-tuple-element.23.own_ref, bf16[768,2560]{1,0:T(8,128)(2,1)} %collective-permute-done.13.main_ref, f32[1,5120]{1,0:T(1,128)} %gain_ref.3, ...), custom_call_target="tpu_custom_call" | custom-call | flops 3932160 | bytes 11796480 | tf_op jit(solution)/shard_map/pallas_call | solution.py:115
  256.5 10.0 %collective-permute-done.20.refs_11_ = bf16[3,640,128]{2,1,0:T(8,128)(2,1)} collective-permute-done((bf16[3,640,128]{2,1,0:T(8,128)(2,1)}, bf16[3,640,128]{2,1,0:T(8,128)(2,1)}, u32[]{:S(2)}, u32[]{:S(2)}) %collective-permute-start.20) | collective-permute-done | bytes 491552 | tf_op jit(solution)/shard_map/ppermute | solution.py:34
  268.5 14.1 %project.3 = (bf16[2,768,128]{2,1,0:T(8,128)(2,1)}, bf16[2,768,256]{2,1,0:T(8,128)(2,1)}) custom-call(s32[5]{0:T(128)} %pad_add_fusion.2.place_ref, bf16[768,2560]{1,0:T(8,128)(2,1)} %shard_map.96.refs_0_, bf16[768,2560]{1,0:T(8,128)(2,1)} %shard_map.98.refs_1_, bf16[768,2560]{1,0:T(8,128)(2,1)} %get-tuple-element.24.refs_2_, ...), custom_call_target="tpu_custom_call" | custom-call | flops 6039797760 | bytes 20840448 | tf_op jit(solution)/shard_map/project/pallas_call | solution.py:158
  288.1 10.0 %collective-permute-done.37.refs_11_ = bf16[3,640,128]{2,1,0:T(8,128)(2,1)} collective-permute-done((bf16[3,640,128]{2,1,0:T(8,128)(2,1)}, bf16[3,640,128]{2,1,0:T(8,128)(2,1)}, u32[]{:S(2)}, u32[]{:S(2)}) %collective-permute-start.37) | collective-permute-done | bytes 491552 | tf_op jit(solution)/shard_map/ppermute | solution.py:34
  298.6 14.1 %project.4 = (bf16[2,768,128]{2,1,0:T(8,128)(2,1)}, bf16[2,768,256]{2,1,0:T(8,128)(2,1)}) custom-call(s32[5]{0:T(128)} %pad_add_fusion.2.place_ref, bf16[768,2560]{1,0:T(8,128)(2,1)} %shard_map.96.refs_0_, bf16[768,2560]{1,0:T(8,128)(2,1)} %shard_map.98.refs_1_, bf16[768,2560]{1,0:T(8,128)(2,1)} %get-tuple-element.24.refs_2_, ...), custom_call_target="tpu_custom_call" | custom-call | flops 6039797760 | bytes 20840448 | tf_op jit(solution)/shard_map/project/pallas_call | solution.py:158
  319.1 10.5 %collective-permute-done.52.refs_11_ = bf16[3,640,128]{2,1,0:T(8,128)(2,1)S(1)} collective-permute-done((bf16[3,640,128]{2,1,0:T(8,128)(2,1)}, bf16[3,640,128]{2,1,0:T(8,128)(2,1)S(1)}, u32[]{:S(2)}, u32[]{:S(2)}) %collective-permute-start.52) | collective-permute-done | bytes 491552 | tf_op jit(solution)/shard_map/ppermute | solution.py:34
  330.4 14.1 %project.5 = (bf16[2,768,128]{2,1,0:T(8,128)(2,1)}, bf16[2,768,256]{2,1,0:T(8,128)(2,1)}) custom-call(s32[5]{0:T(128)} %pad_add_fusion.2.place_ref, bf16[768,2560]{1,0:T(8,128)(2,1)} %shard_map.96.refs_0_, bf16[768,2560]{1,0:T(8,128)(2,1)} %shard_map.98.refs_1_, bf16[768,2560]{1,0:T(8,128)(2,1)} %get-tuple-element.24.refs_2_, ...), custom_call_target="tpu_custom_call" | custom-call | flops 6039797760 | bytes 20840448 | tf_op jit(solution)/shard_map/project/pallas_call | solution.py:158
  346.5 7.3 %attend.3 = (bf16[1152,128]{1,0:T(8,128)(2,1)}, bf16[384,128]{1,0:T(8,128)(2,1)}) custom-call(s32[1]{0:T(128)} %bitcast.4.b_ref, bf16[2,768,128]{2,1,0:T(8,128)(2,1)} %get-tuple-element.26.q_ref, bf16[2,768,256]{2,1,0:T(8,128)(2,1)} %get-tuple-element.27.own_ref, bf16[2,768,256]{2,1,0:T(8,128)(2,1)} %collective-permute-done.21.other_ref), custom_call_target="tpu_custom_call" | custom-call | flops 1207959552 | bytes 2359296 | tf_op jit(solution)/shard_map/attend/pallas_call | solution.py:227
  355.1 8.3 %collective-permute-done.38.other_ref = bf16[2,768,256]{2,1,0:T(8,128)(2,1)} collective-permute-done((bf16[2,768,256]{2,1,0:T(8,128)(2,1)}, bf16[2,768,256]{2,1,0:T(8,128)(2,1)}, u32[]{:S(2)}, u32[]{:S(2)}) %collective-permute-start.38) | collective-permute-done | bytes 786464 | tf_op jit(solution)/shard_map/ppermute | solution.py:34
  363.4 7.3 %attend.4 = (bf16[1152,128]{1,0:T(8,128)(2,1)}, bf16[384,128]{1,0:T(8,128)(2,1)}) custom-call(s32[1]{0:T(128)} %bitcast.4.b_ref, bf16[2,768,128]{2,1,0:T(8,128)(2,1)} %get-tuple-element.30.q_ref, bf16[2,768,256]{2,1,0:T(8,128)(2,1)} %get-tuple-element.31.own_ref, bf16[2,768,256]{2,1,0:T(8,128)(2,1)} %collective-permute-done.38.other_ref), custom_call_target="tpu_custom_call" | custom-call | flops 1207959552 | bytes 2359296 | tf_op jit(solution)/shard_map/attend/pallas_call | solution.py:227
  378.7 7.3 %attend.5 = (bf16[1152,128]{1,0:T(8,128)(2,1)}, bf16[384,128]{1,0:T(8,128)(2,1)}) custom-call(s32[1]{0:T(128)} %bitcast.4.b_ref, bf16[2,768,128]{2,1,0:T(8,128)(2,1)} %get-tuple-element.34.q_ref, bf16[2,768,256]{2,1,0:T(8,128)(2,1)} %get-tuple-element.35.own_ref, bf16[2,768,256]{2,1,0:T(8,128)(2,1)} %copy-done.25), custom_call_target="tpu_custom_call" | custom-call | flops 1207959552 | bytes 2359296 | tf_op jit(solution)/shard_map/attend/pallas_call | solution.py:227
  394.7 12.1 %collective-permute-start.42 = (bf16[1152,128]{1,0:T(8,128)(2,1)S(1)}, bf16[1152,128]{1,0:T(8,128)(2,1)S(1)}, u32[]{:S(2)}, u32[]{:S(2)}) collective-permute-start(bf16[1152,128]{1,0:T(8,128)(2,1)S(1)} %select_dynamic-update-slice_fusion.1.refs_0_), channel_id=1, source_target_pairs={{0,12},{4,0},{8,4},{12,8},{1,13},{5,1},{9,5},{13,9},{2,14},{6,2},{... | collective-permute-start | bytes 884744 | tf_op jit(solution)/shard_map/ppermute | solution.py:39
  412.8 7.1 %collective-permute-done.40.refs_1_ = bf16[1152,128]{1,0:T(8,128)(2,1)S(1)} collective-permute-done((bf16[1152,128]{1,0:T(8,128)(2,1)S(1)}, bf16[1152,128]{1,0:T(8,128)(2,1)S(1)}, u32[]{:S(2)}, u32[]{:S(2)}) %collective-permute-start.40) | collective-permute-done | bytes 294944 | tf_op jit(solution)/shard_map/ppermute | solution.py:39
  419.9 9.8 %collective-permute-done.41.refs_2_ = bf16[1152,128]{1,0:T(8,128)(2,1)S(1)} collective-permute-done((bf16[1152,128]{1,0:T(8,128)(2,1)S(1)}, bf16[1152,128]{1,0:T(8,128)(2,1)S(1)}, u32[]{:S(2)}, u32[]{:S(2)}) %collective-permute-start.41) | collective-permute-done | bytes 294944 | tf_op jit(solution)/shard_map/ppermute | solution.py:39
  437.8 7.4 %collective-permute-done.55.refs_9_ = bf16[1152,128]{1,0:T(8,128)(2,1)S(1)} collective-permute-done((bf16[1152,128]{1,0:T(8,128)(2,1)}, bf16[1152,128]{1,0:T(8,128)(2,1)S(1)}, u32[]{:S(2)}, u32[]{:S(2)}) %collective-permute-start.55) | collective-permute-done | bytes 294944 | tf_op jit(solution)/shard_map/ppermute | solution.py:39
  488.0 7.0 %project_out.4.refs_16_ = f32[768,640]{1,0:T(8,128)} custom-call(s32[5]{0:T(128)} %pad_add_fusion.1.at_ref, bf16[1152,128]{1,0:T(8,128)(2,1)} %copy-done.5, bf16[1152,128]{1,0:T(8,128)(2,1)} %copy-done.8, bf16[1152,128]{1,0:T(8,128)(2,1)} %copy-done.9, bf16[1152,128]{1,0:T(8,128)(2,1)} %copy-done.10, bf16[1152,128]{1,0:T(8,128)(2,1)} %copy-done.11, ...), custom_call_target="tpu_custom_call" | custom-call | flops 2013265920 | bytes 9699328 | tf_op jit(solution)/shard_map/project_out/pallas_call | solution.py:280
  527.1 9.9 %collective-permute-start.66 = (bf16[2,192,640]{2,1,0:T(8,128)(2,1)S(1)}, bf16[2,192,640]{2,1,0:T(8,128)(2,1)S(1)}, u32[]{:S(2)}, u32[]{:S(2)}) collective-permute-start(bf16[2,192,640]{2,1,0:T(8,128)(2,1)S(1)} %get-tuple-element.54), channel_id=1, source_target_pairs={{0,0},{1,4},{4,1},{5,5},{8,16},{9,20},{12,17},{13,21},{16,8},{17,1... | collective-permute-start | bytes 1474568 | tf_op jit(solution)/shard_map/ppermute | solution.py:410
  537.0 7.2 %collective-permute-done.65 = bf16[2,192,640]{2,1,0:T(8,128)(2,1)S(1)} collective-permute-done((bf16[2,192,640]{2,1,0:T(8,128)(2,1)S(1)}, bf16[2,192,640]{2,1,0:T(8,128)(2,1)S(1)}, u32[]{:S(2)}, u32[]{:S(2)}) %collective-permute-start.65) | collective-permute-done | bytes 491552 | tf_op jit(solution)/shard_map/ppermute | solution.py:410
  544.2 13.3 %collective-permute-done.66 = bf16[2,192,640]{2,1,0:T(8,128)(2,1)S(1)} collective-permute-done((bf16[2,192,640]{2,1,0:T(8,128)(2,1)S(1)}, bf16[2,192,640]{2,1,0:T(8,128)(2,1)S(1)}, u32[]{:S(2)}, u32[]{:S(2)}) %collective-permute-start.66) | collective-permute-done | bytes 491552 | tf_op jit(solution)/shard_map/ppermute | solution.py:410
  (192 shorter events, 203.3 us)
Async XLA Ops:
  38.4 27.9 %collective-permute-start.7 = (bf16[192,2560]{1,0:T(8,128)(2,1)S(1)}, bf16[192,2560]{1,0:T(8,128)(2,1)S(1)}, u32[]{:S(2)}, u32[]{:S(2)}) collective-permute-start(bf16[192,2560]{1,0:T(8,128)(2,1)S(1)} %collective-permute-done.refs_1_), channel_id=1, source_target_pairs={{0,1},{1,0},{4,5},{5,4},{8,9},{9,8},{2,3},{3,2},{6,7},{7,6},{10,11... | collective-permute-start | bytes 2949128 | tf_op jit(solution)/shard_map/ppermute | solution.py:346
  62.1 28.8 %collective-permute-start.12 = (bf16[192,2560]{1,0:T(8,128)(2,1)S(1)}, bf16[192,2560]{1,0:T(8,128)(2,1)}, u32[]{:S(2)}, u32[]{:S(2)}) collective-permute-start(bf16[192,2560]{1,0:T(8,128)(2,1)S(1)} %collective-permute-done.1.refs_6_), channel_id=1, source_target_pairs={{4,5},{5,4},{8,9},{9,8},{12,13},{13,12},{6,7},{7,6},{10,11},{11,10... | collective-permute-start | bytes 2949128 | tf_op jit(solution)/shard_map/ppermute | solution.py:345
  64.6 29.5 %collective-permute-start.9 = (bf16[192,2560]{1,0:T(8,128)(2,1)}, bf16[192,2560]{1,0:T(8,128)(2,1)}, u32[]{:S(2)}, u32[]{:S(2)}) collective-permute-start(bf16[192,2560]{1,0:T(8,128)(2,1)} %collective-permute-done.4.refs_3_), channel_id=1, source_target_pairs={{0,1},{1,0},{4,5},{5,4},{2,3},{3,2},{6,7},{7,6},{16,17},{17,16},{2... | collective-permute-start | bytes 2949128 | tf_op jit(solution)/shard_map/ppermute | solution.py:346
  66.2 40.5 %collective-permute-start.10 = (bf16[192,2560]{1,0:T(8,128)(2,1)S(1)}, bf16[192,2560]{1,0:T(8,128)(2,1)}, u32[]{:S(2)}, u32[]{:S(2)}) collective-permute-start(bf16[192,2560]{1,0:T(8,128)(2,1)S(1)} %collective-permute-done.2.refs_4_), channel_id=1, source_target_pairs={{8,9},{9,8},{12,13},{13,12},{10,11},{11,10},{14,15},{15,14},{24,25... | collective-permute-start | bytes 2949128 | tf_op jit(solution)/shard_map/ppermute | solution.py:345
  78.8 27.9 %collective-permute-start.8 = (bf16[192,2560]{1,0:T(8,128)(2,1)}, bf16[192,2560]{1,0:T(8,128)(2,1)}, u32[]{:S(2)}, u32[]{:S(2)}) collective-permute-start(bf16[192,2560]{1,0:T(8,128)(2,1)} %collective-permute-done.3.refs_2_), channel_id=1, source_target_pairs={{12,13},{13,12},{14,15},{15,14},{28,29},{29,28},{30,31},{31,30}} | collective-permute-start | bytes 2949128 | tf_op jit(solution)/shard_map/ppermute | solution.py:345
  90.9 140.6 %collective-permute-start.6 = (bf16[768,2560]{1,0:T(8,128)(2,1)}, bf16[768,2560]{1,0:T(8,128)(2,1)}, u32[]{:S(2)}, u32[]{:S(2)}) collective-permute-start(bf16[768,2560]{1,0:T(8,128)(2,1)} %get-tuple-element.21.own_ref), channel_id=1, source_target_pairs={{0,16},{1,17},{2,18},{3,19},{4,20},{5,21},{6,22},{7,23},{8,24},{9,... | collective-permute-start | bytes 11796488 | tf_op jit(solution)/shard_map/ppermute | solution.py:358
  114.4 118.7 %collective-permute-start.13 = (bf16[768,2560]{1,0:T(8,128)(2,1)}, bf16[768,2560]{1,0:T(8,128)(2,1)}, u32[]{:S(2)}, u32[]{:S(2)}) collective-permute-start(bf16[768,2560]{1,0:T(8,128)(2,1)} %get-tuple-element.23.own_ref), channel_id=1, source_target_pairs={{0,16},{1,17},{2,18},{3,19},{4,20},{5,21},{6,22},{7,23},{8,24},{9,... | collective-permute-start | bytes 11796488 | tf_op jit(solution)/shard_map/ppermute | solution.py:358
  121.5 28.1 %collective-permute-start.15 = (bf16[3,640,128]{2,1,0:T(8,128)(2,1)S(1)}, bf16[3,640,128]{2,1,0:T(8,128)(2,1)}, u32[]{:S(2)}, u32[]{:S(2)}) collective-permute-start(bf16[3,640,128]{2,1,0:T(8,128)(2,1)S(1)} %get-tuple-element.47), channel_id=1, source_target_pairs={{0,4},{4,8},{8,12},{12,0},{1,5},{5,9},{9,13},{13,1},{2,6},{6,10},{... | collective-permute-start | bytes 1474568 | tf_op jit(solution)/shard_map/ppermute | solution.py:39
  141.3 89.7 %collective-permute-start.30 = (bf16[1536,640]{1,0:T(8,128)(2,1)S(1)}, bf16[1536,640]{1,0:T(8,128)(2,1)}, u32[]{:S(2)}, u32[]{:S(2)}) collective-permute-start(bf16[1536,640]{1,0:T(8,128)(2,1)S(1)} %bitcast.59), channel_id=1, source_target_pairs={{0,2},{2,0},{1,3},{3,1},{4,6},{6,4},{5,7},{7,5},{8,10},{10,8},{9,1... | collective-permute-start | bytes 5898248 | tf_op jit(solution)/shard_map/ppermute | solution.py:34
  149.6 39.7 %collective-permute-start.19 = (bf16[3,640,128]{2,1,0:T(8,128)(2,1)S(1)}, bf16[3,640,128]{2,1,0:T(8,128)(2,1)}, u32[]{:S(2)}, u32[]{:S(2)}) collective-permute-start(bf16[3,640,128]{2,1,0:T(8,128)(2,1)S(1)} %get-tuple-element.45), channel_id=1, source_target_pairs={{0,12},{4,0},{8,4},{12,8},{1,13},{5,1},{9,5},{13,9},{2,14},{6,2},{... | collective-permute-start | bytes 1474568 | tf_op jit(solution)/shard_map/ppermute | solution.py:39
  192.0 75.0 %collective-permute-start.14 = (bf16[3,640,384]{2,1,0:T(8,128)(2,1)}, bf16[3,640,384]{2,1,0:T(8,128)(2,1)S(1)}, u32[]{:S(2)}, u32[]{:S(2)}) collective-permute-start(bf16[3,640,384]{2,1,0:T(8,128)(2,1)} %dynamic-slice_bitcast_fusion), channel_id=1, source_target_pairs={{0,2},{2,0},{1,3},{3,1},{4,6},{6,4},{5,7},{7,5},{8,10},{10,8},{9,1... | collective-permute-start | bytes 4423688 | tf_op jit(solution)/shard_map/ppermute | solution.py:34
  233.0 33.4 %collective-permute-start.20 = (bf16[3,640,128]{2,1,0:T(8,128)(2,1)}, bf16[3,640,128]{2,1,0:T(8,128)(2,1)}, u32[]{:S(2)}, u32[]{:S(2)}) collective-permute-start(bf16[3,640,128]{2,1,0:T(8,128)(2,1)} %collective-permute-done.19.refs_10_), channel_id=1, source_target_pairs={{0,2},{2,0},{1,3},{3,1},{4,6},{6,4},{5,7},{7,5},{8,10},{10,8},{9,1... | collective-permute-start | bytes 1474568 | tf_op jit(solution)/shard_map/ppermute | solution.py:34
  250.7 31.9 %collective-permute-start.49 = (bf16[3,640,128]{2,1,0:T(8,128)(2,1)}, bf16[3,640,128]{2,1,0:T(8,128)(2,1)}, u32[]{:S(2)}, u32[]{:S(2)}) collective-permute-start(bf16[3,640,128]{2,1,0:T(8,128)(2,1)} %get-tuple-element.48), channel_id=1, source_target_pairs={{0,8},{4,12},{8,0},{12,4},{1,9},{5,13},{9,1},{13,5},{2,10},{6,14},... | collective-permute-start | bytes 1474568 | tf_op jit(solution)/shard_map/ppermute | solution.py:39
  250.7 33.1 %collective-permute-start.51 = (bf16[3,640,128]{2,1,0:T(8,128)(2,1)}, bf16[3,640,128]{2,1,0:T(8,128)(2,1)}, u32[]{:S(2)}, u32[]{:S(2)}) collective-permute-start(bf16[3,640,128]{2,1,0:T(8,128)(2,1)} %get-tuple-element.40), channel_id=1, source_target_pairs={{0,12},{4,0},{8,4},{12,8},{1,13},{5,1},{9,5},{13,9},{2,14},{6,2},{... | collective-permute-start | bytes 1474568 | tf_op jit(solution)/shard_map/ppermute | solution.py:39
  256.0 28.8 %collective-permute-start.33 = (bf16[3,640,128]{2,1,0:T(8,128)(2,1)}, bf16[3,640,128]{2,1,0:T(8,128)(2,1)}, u32[]{:S(2)}, u32[]{:S(2)}) collective-permute-start(bf16[3,640,128]{2,1,0:T(8,128)(2,1)} %collective-permute-done.32.refs_6_), channel_id=1, source_target_pairs={{0,2},{2,0},{1,3},{3,1},{4,6},{6,4},{5,7},{7,5},{8,10},{10,8},{9,1... | collective-permute-start | bytes 1474568 | tf_op jit(solution)/shard_map/ppermute | solution.py:34
  267.0 31.1 %collective-permute-start.37 = (bf16[3,640,128]{2,1,0:T(8,128)(2,1)}, bf16[3,640,128]{2,1,0:T(8,128)(2,1)}, u32[]{:S(2)}, u32[]{:S(2)}) collective-permute-start(bf16[3,640,128]{2,1,0:T(8,128)(2,1)} %collective-permute-done.36.refs_10_), channel_id=1, source_target_pairs={{0,2},{2,0},{1,3},{3,1},{4,6},{6,4},{5,7},{7,5},{8,10},{10,8},{9,1... | collective-permute-start | bytes 1474568 | tf_op jit(solution)/shard_map/ppermute | solution.py:34
  282.7 30.1 %collective-permute-start.48 = (bf16[3,640,128]{2,1,0:T(8,128)(2,1)}, bf16[3,640,128]{2,1,0:T(8,128)(2,1)S(1)}, u32[]{:S(2)}, u32[]{:S(2)}) collective-permute-start(bf16[3,640,128]{2,1,0:T(8,128)(2,1)} %collective-permute-done.47.refs_6_), channel_id=1, source_target_pairs={{0,2},{2,0},{1,3},{3,1},{4,6},{6,4},{5,7},{7,5},{8,10},{10,8},{9,1... | collective-permute-start | bytes 1474568 | tf_op jit(solution)/shard_map/ppermute | solution.py:34
  283.8 35.2 %collective-permute-start.50 = (bf16[3,640,128]{2,1,0:T(8,128)(2,1)}, bf16[3,640,128]{2,1,0:T(8,128)(2,1)S(1)}, u32[]{:S(2)}, u32[]{:S(2)}) collective-permute-start(bf16[3,640,128]{2,1,0:T(8,128)(2,1)} %collective-permute-done.49.refs_8_), channel_id=1, source_target_pairs={{0,2},{2,0},{1,3},{3,1},{4,6},{6,4},{5,7},{7,5},{8,10},{10,8},{9,1... | collective-permute-start | bytes 1474568 | tf_op jit(solution)/shard_map/ppermute | solution.py:34
  284.8 44.8 %collective-permute-start.52 = (bf16[3,640,128]{2,1,0:T(8,128)(2,1)}, bf16[3,640,128]{2,1,0:T(8,128)(2,1)S(1)}, u32[]{:S(2)}, u32[]{:S(2)}) collective-permute-start(bf16[3,640,128]{2,1,0:T(8,128)(2,1)} %collective-permute-done.51.refs_10_), channel_id=1, source_target_pairs={{0,2},{2,0},{1,3},{3,1},{4,6},{6,4},{5,7},{7,5},{8,10},{10,8},{9,1... | collective-permute-start | bytes 1474568 | tf_op jit(solution)/shard_map/ppermute | solution.py:34
  287.6 98.5 %collective-permute-start.31 = (bf16[1536,640]{1,0:T(8,128)(2,1)}, bf16[1536,640]{1,0:T(8,128)(2,1)}, u32[]{:S(2)}, u32[]{:S(2)}) collective-permute-start(bf16[1536,640]{1,0:T(8,128)(2,1)} %get-tuple-element.49), channel_id=1, source_target_pairs={{0,1},{1,0},{2,3},{3,2},{4,5},{5,4},{6,7},{7,6},{8,9},{9,8},{10,11... | collective-permute-start | bytes 5898248 | tf_op jit(solution)/shard_map/ppermute | solution.py:34
  298.1 48.5 %collective-permute-start.21 = (bf16[2,768,256]{2,1,0:T(8,128)(2,1)}, bf16[2,768,256]{2,1,0:T(8,128)(2,1)}, u32[]{:S(2)}, u32[]{:S(2)}) collective-permute-start(bf16[2,768,256]{2,1,0:T(8,128)(2,1)} %get-tuple-element.27.own_ref), channel_id=1, source_target_pairs={{0,2},{2,0},{1,3},{3,1},{4,6},{6,4},{5,7},{7,5},{8,10},{10,8},{9,1... | collective-permute-start | bytes 2359304 | tf_op jit(solution)/shard_map/ppermute | solution.py:34
  312.7 50.7 %collective-permute-start.38 = (bf16[2,768,256]{2,1,0:T(8,128)(2,1)}, bf16[2,768,256]{2,1,0:T(8,128)(2,1)}, u32[]{:S(2)}, u32[]{:S(2)}) collective-permute-start(bf16[2,768,256]{2,1,0:T(8,128)(2,1)} %get-tuple-element.31.own_ref), channel_id=1, source_target_pairs={{0,2},{2,0},{1,3},{3,1},{4,6},{6,4},{5,7},{7,5},{8,10},{10,8},{9,1... | collective-permute-start | bytes 2359304 | tf_op jit(solution)/shard_map/ppermute | solution.py:34
  344.5 33.3 %collective-permute-start.53 = (bf16[2,768,256]{2,1,0:T(8,128)(2,1)}, bf16[2,768,256]{2,1,0:T(8,128)(2,1)S(1)}, u32[]{:S(2)}, u32[]{:S(2)}) collective-permute-start(bf16[2,768,256]{2,1,0:T(8,128)(2,1)} %get-tuple-element.35.own_ref), channel_id=1, source_target_pairs={{0,2},{2,0},{1,3},{3,1},{4,6},{6,4},{5,7},{7,5},{8,10},{10,8},{9,1... | collective-permute-start | bytes 2359304 | tf_op jit(solution)/shard_map/ppermute | solution.py:34
  377.8 32.8 %collective-permute-start.25 = (bf16[1152,128]{1,0:T(8,128)(2,1)S(1)}, bf16[1152,128]{1,0:T(8,128)(2,1)}, u32[]{:S(2)}, u32[]{:S(2)}) collective-permute-start(bf16[1152,128]{1,0:T(8,128)(2,1)S(1)} %select_dynamic-update-slice_fusion.2.refs_0_), channel_id=1, source_target_pairs={{0,12},{4,0},{8,4},{12,8},{1,13},{5,1},{9,5},{13,9},{2,14},{6,2},{... | collective-permute-start | bytes 884744 | tf_op jit(solution)/shard_map/ppermute | solution.py:39
  389.4 30.5 %collective-permute-start.40 = (bf16[1152,128]{1,0:T(8,128)(2,1)S(1)}, bf16[1152,128]{1,0:T(8,128)(2,1)S(1)}, u32[]{:S(2)}, u32[]{:S(2)}) collective-permute-start(bf16[1152,128]{1,0:T(8,128)(2,1)S(1)} %select_dynamic-update-slice_fusion.1.refs_0_), channel_id=1, source_target_pairs={{0,4},{4,8},{8,12},{12,0},{1,5},{5,9},{9,13},{13,1},{2,6},{6,10},{... | collective-permute-start | bytes 884744 | tf_op jit(solution)/shard_map/ppermute | solution.py:39
  394.7 35.0 %collective-permute-start.41 = (bf16[1152,128]{1,0:T(8,128)(2,1)S(1)}, bf16[1152,128]{1,0:T(8,128)(2,1)S(1)}, u32[]{:S(2)}, u32[]{:S(2)}) collective-permute-start(bf16[1152,128]{1,0:T(8,128)(2,1)S(1)} %select_dynamic-update-slice_fusion.1.refs_0_), channel_id=1, source_target_pairs={{0,8},{4,12},{8,0},{12,4},{1,9},{5,13},{9,1},{13,5},{2,10},{6,14},... | collective-permute-start | bytes 884744 | tf_op jit(solution)/shard_map/ppermute | solution.py:39
  394.7 41.3 %collective-permute-start.42 = (bf16[1152,128]{1,0:T(8,128)(2,1)S(1)}, bf16[1152,128]{1,0:T(8,128)(2,1)S(1)}, u32[]{:S(2)}, u32[]{:S(2)}) collective-permute-start(bf16[1152,128]{1,0:T(8,128)(2,1)S(1)} %select_dynamic-update-slice_fusion.1.refs_0_), channel_id=1, source_target_pairs={{0,12},{4,0},{8,4},{12,8},{1,13},{5,1},{9,5},{13,9},{2,14},{6,2},{... | collective-permute-start | bytes 884744 | tf_op jit(solution)/shard_map/ppermute | solution.py:39
  412.7 32.4 %collective-permute-start.55 = (bf16[1152,128]{1,0:T(8,128)(2,1)}, bf16[1152,128]{1,0:T(8,128)(2,1)S(1)}, u32[]{:S(2)}, u32[]{:S(2)}) collective-permute-start(bf16[1152,128]{1,0:T(8,128)(2,1)} %select_dynamic-update-slice_fusion.refs_8_), channel_id=1, source_target_pairs={{0,4},{4,8},{8,12},{12,0},{1,5},{5,9},{9,13},{13,1},{2,6},{6,10},{... | collective-permute-start | bytes 884744 | tf_op jit(solution)/shard_map/ppermute | solution.py:39
  419.9 26.6 %collective-permute-start.56 = (bf16[1152,128]{1,0:T(8,128)(2,1)}, bf16[1152,128]{1,0:T(8,128)(2,1)}, u32[]{:S(2)}, u32[]{:S(2)}) collective-permute-start(bf16[1152,128]{1,0:T(8,128)(2,1)} %select_dynamic-update-slice_fusion.refs_8_), channel_id=1, source_target_pairs={{0,8},{4,12},{8,0},{12,4},{1,9},{5,13},{9,1},{13,5},{2,10},{6,14},... | collective-permute-start | bytes 884744 | tf_op jit(solution)/shard_map/ppermute | solution.py:39
  436.5 78.1 %collective-permute-start.63 = (bf16[1536,640]{1,0:T(8,128)(2,1)S(1)}, bf16[1536,640]{1,0:T(8,128)(2,1)}, u32[]{:S(2)}, u32[]{:S(2)}) collective-permute-start(bf16[1536,640]{1,0:T(8,128)(2,1)S(1)} %get-tuple-element.50.refs_16_.refs_17_.refs_18_.refs_19_.refs_24_.refs_25_.refs_26_.refs_27_.refs_8_.refs_9_.re, ...), channel_id=1, source_target_pairs={{16,0},{17,1},{18,2},{19,3},{20,4},{21,5},{22,6},{23,7},{24,8},{25... | collective-permute-start | bytes 5898248 | tf_op jit(solution)/shard_map/ppermute | solution.py:371
  445.2 69.4 %collective-permute-start.64 = (bf16[1536,640]{1,0:T(8,128)(2,1)}, bf16[1536,640]{1,0:T(8,128)(2,1)}, u32[]{:S(2)}, u32[]{:S(2)}) collective-permute-start(bf16[1536,640]{1,0:T(8,128)(2,1)} %collective-permute-done.31.refs_20_.refs_21_.refs_22_.refs_23_.refs_28_.refs_29_.refs_30_.refs_31_.refs_12_.refs_13_.re, ...), channel_id=1, source_target_pairs={{16,0},{17,1},{18,2},{19,3},{20,4},{21,5},{22,6},{23,7},{24,8},{25... | collective-permute-start | bytes 5898248 | tf_op jit(solution)/shard_map/ppermute | solution.py:371
  527.1 30.3 %collective-permute-start.66 = (bf16[2,192,640]{2,1,0:T(8,128)(2,1)S(1)}, bf16[2,192,640]{2,1,0:T(8,128)(2,1)S(1)}, u32[]{:S(2)}, u32[]{:S(2)}) collective-permute-start(bf16[2,192,640]{2,1,0:T(8,128)(2,1)S(1)} %get-tuple-element.54), channel_id=1, source_target_pairs={{0,0},{1,4},{4,1},{5,5},{8,16},{9,20},{12,17},{13,21},{16,8},{17,1... | collective-permute-start | bytes 1474568 | tf_op jit(solution)/shard_map/ppermute | solution.py:410
  (62 other events, 1586.8 us)

commit v2 on v1

--- a/solution.py
+++ b/solution.py
@@ -252,7 +252,7 @@
     )(b, q, own, other)
 
 
-def project_out_kernel(count, choices, first, at_ref, *refs):
+def project_out_kernel(count, choices, first, split, at_ref, *refs):
     pieces, weights = refs[:count], refs[count : (1 + choices) * count]
     rows = jnp.concatenate([a[...] for a in pieces], axis=1)
     weight = jnp.concatenate([w[...] for w in weights[:count]], axis=0)
@@ -260,10 +260,23 @@
         other = jnp.concatenate([w[...] for w in weights[count:]], axis=0)
         weight = jnp.where(at_ref[at_ref.shape[0] - 1] == 0, weight, other)
     total = jnp.dot(rows, weight, preferred_element_type=jnp.float32)
-    refs[-1][...] = total if first else refs[-2][...] + total
-
-
-def project_out(sets, tiles, places, choices, carry):
+    if not first:
+        total = refs[-3 if split else -2][...] + total
+    if not split:
+        refs[-1][...] = total
+        return
+    kept = pl.program_id(0) == at_ref[at_ref.shape[0] - 1]
+
+    @pl.when(kept)
+    def _():
+        refs[-2][...] = total
+
+    @pl.when(jnp.logical_not(kept))
+    def _():
+        refs[-1][...] = total
+
+
+def project_out(sets, tiles, places, choices, carry, split=False):
     tile = sets[0][1][0].shape[0] // 3
     each = len(sets[0][1]) // 2
     count = 2 * each * len(sets)
@@ -278,7 +291,7 @@
     weight_specs = [weight_spec(k % each, head) for head, _ in sets for k in range(2 * each)]
     o_spec = pl.BlockSpec((tile, width), lambda t, at: (t, 0))
     return pl.pallas_call(
-        functools.partial(project_out_kernel, count, len(choices), first),
+        functools.partial(project_out_kernel, count, len(choices), first, split),
         name="project_out",
         grid_spec=pltpu.PrefetchScalarGridSpec(
             num_scalar_prefetch=1,
@@ -286,9 +299,13 @@
             in_specs=[pl.BlockSpec((tile, HD), lambda t, at: (t + lo, 0))] * count
             + weight_specs * len(choices)
             + ([] if first else [o_spec]),
-            out_specs=o_spec,
-        ),
-        out_shape=jax.ShapeDtypeStruct((rows, width), jnp.float32),
+            out_specs=[pl.BlockSpec((tile, width), lambda t, at: (0, 0))] * 2
+            if split
+            else o_spec,
+        ),
+        out_shape=[jax.ShapeDtypeStruct((tile, width), jnp.float32)] * 2
+        if split
+        else jax.ShapeDtypeStruct((rows, width), jnp.float32),
         cost_estimate=pl.CostEstimate(
             flops=2 * rows * width * HD * count,
             transcendentals=0,
@@ -386,11 +403,9 @@
     main_only, either = (out_own,), (out_critic, out_own)
     early = project_out(sets[:-1], (0, 2), out_places, main_only, None)
     early_own = project_out(sets[:-1], (2, 3), out_places, either, None)
-    pred = project_out(sets[-1:], (0, 2), out_places, main_only, early)
+    kept, given = project_out(sets[-1:], (0, 2), out_places, main_only, early, split=True)
     own_pred = project_out(sets[-1:], (2, 3), out_places, either, early_own)
 
-    kept = lax.dynamic_slice_in_dim(pred, b * (rows // 2), rows // 2, 0)
-    given = lax.dynamic_slice_in_dim(pred, (1 - b) * (rows // 2), rows // 2, 0)
     given = swap(given, "branch")
     dmd = jnp.where(b == 0, given - kept, kept - given)
     value = jnp.stack([dmd, own_pred]).astype(jnp.bfloat16)

time: 563 us -> 561 us (level)
  no operation moved by 1% of the time
where the time goes in v2:
time: 561 us; the launch traced here: 560 us
  waiting for transfers between devices  290 us (52%)
  starting transfers between devices  123 us (22%)
  Pallas kernels  121 us (22%)
  local copies, waits for them, and re-layouts  12.1 us (2%)
  other arithmetic  12 us (2%)
    ppermute x18, waiting for transfers between devices, shift(): lax.ppermute(x, axis, [(i, (i + distance) % size) for i in range(size)])  112 us
    ppermute x28, waiting for transfers between devices, swap(): return lax.ppermute(x, axis, [(0, 1), (1, 0)])  99.6 us
    ppermute x18, starting transfers between devices, shift(): lax.ppermute(x, axis, [(i, (i + distance) % size) for i in range(size)])  47.4 us
    ppermute x3, waiting for transfers between devices, split_step(): lax.ppermute(ups[-1][0], 'outer', [(i, i + 1) for i in range(k - 1, nz -...  44.1 us
    pallas_call x3, Pallas kernels, project(): pl.pallas_call(project_kernel, name='project', grid_spec=pltpu.PrefetchSc...  42.5 us
    pallas_call x4, Pallas kernels, columns(): pl.pallas_call(kernel, grid_spec=pltpu.PrefetchScalarGridSpec(num_scalar_...  28.7 us
    pallas_call x4, Pallas kernels, project_out(): pl.pallas_call(functools.partial(project_out_kernel, count, len(choices),...  23.7 us
    pallas_call x3, Pallas kernels, attend(): pl.pallas_call(attend_kernel, name='attend', grid_spec=pltpu.PrefetchScal...  22 us
  transfers between devices with their start and end apart: 67, of which 36 were waited for; matrix products, arithmetic and copies ran while one was open for 3% of the time, Pallas kernels for 21%

profile of v2, /device:TPU:22, one launch (start us, length us, event | category | flops | bytes accessed | tf_op | source)
XLA Modules:
  0.0 559.9 jit_solution(15569578311837640046)
XLA Ops:
  11.7 19.7 %collective-permute-done.1.refs_6_ = bf16[192,2560]{1,0:T(8,128)(2,1)S(1)} collective-permute-done((bf16[192,2560]{1,0:T(8,128)(2,1)}, bf16[192,2560]{1,0:T(8,128)(2,1)S(1)}, u32[]{:S(2)}, u32[]{:S(2)}) %collective-permute-start.1) | collective-permute-done | bytes 983072 | tf_op jit(solution)/shard_map/ppermute | solution.py:359
  40.8 15.2 %collective-permute-done.2.refs_4_ = bf16[192,2560]{1,0:T(8,128)(2,1)S(1)} collective-permute-done((bf16[192,2560]{1,0:T(8,128)(2,1)S(1)}, bf16[192,2560]{1,0:T(8,128)(2,1)S(1)}, u32[]{:S(2)}, u32[]{:S(2)}) %collective-permute-start.2) | collective-permute-done | bytes 983072 | tf_op jit(solution)/shard_map/ppermute | solution.py:359
  69.6 9.2 %collective-permute-done.3.refs_2_ = bf16[192,2560]{1,0:T(8,128)(2,1)} collective-permute-done((bf16[192,2560]{1,0:T(8,128)(2,1)S(1)}, bf16[192,2560]{1,0:T(8,128)(2,1)}, u32[]{:S(2)}, u32[]{:S(2)}) %collective-permute-start.3) | collective-permute-done | bytes 983072 | tf_op jit(solution)/shard_map/ppermute | solution.py:359
  83.4 7.7 %shard_map.95 = (bf16[768,2560]{1,0:T(8,128)(2,1)}, bf16[768,2560]{1,0:T(8,128)(2,1)}) custom-call(s32[1]{0:T(128)} %bitcast.4.b_ref, s32[4]{0:T(128)} %pad_add_fusion.3.at_ref, s32[2]{0:T(128)} %cfg_ref.7, s32[1]{0:T(128)} %bitcast.10.z_ref, bf16[192,2560]{1,0:T(8,128)(2,1)} %get-tuple-element.22.refs_0_, bf16[192,2560]{1,0:T(8,128)(2,1)} %copy-done.26, ...), custom_call_target="tpu_custom_call" | custom-call | flops 3932160 | bytes 11796480 | tf_op jit(solution)/shard_map/pallas_call | solution.py:115
  94.2 12.5 %collective-permute-done.10.refs_4_ = bf16[192,2560]{1,0:T(8,128)(2,1)} collective-permute-done((bf16[192,2560]{1,0:T(8,128)(2,1)S(1)}, bf16[192,2560]{1,0:T(8,128)(2,1)}, u32[]{:S(2)}, u32[]{:S(2)}) %collective-permute-start.10) | collective-permute-done | bytes 983072 | tf_op jit(solution)/shard_map/ppermute | solution.py:362
  106.7 7.7 %shard_map.97 = (bf16[768,2560]{1,0:T(8,128)(2,1)}, bf16[768,2560]{1,0:T(8,128)(2,1)}) custom-call(s32[1]{0:T(128)} %bitcast.4.b_ref, s32[4]{0:T(128)} %pad_add_fusion.4.at_ref, s32[2]{0:T(128)} %cfg_ref.7, s32[1]{0:T(128)} %bitcast.10.z_ref, bf16[192,2560]{1,0:T(8,128)(2,1)} %get-tuple-element.24.refs_0_, bf16[192,2560]{1,0:T(8,128)(2,1)} %copy-done.23, ...), custom_call_target="tpu_custom_call" | custom-call | flops 3932160 | bytes 11796480 | tf_op jit(solution)/shard_map/pallas_call | solution.py:115
  121.5 19.8 %collective-permute-start.15 = (bf16[3,640,128]{2,1,0:T(8,128)(2,1)S(1)}, bf16[3,640,128]{2,1,0:T(8,128)(2,1)}, u32[]{:S(2)}, u32[]{:S(2)}) collective-permute-start(bf16[3,640,128]{2,1,0:T(8,128)(2,1)S(1)} %get-tuple-element.51), channel_id=1, source_target_pairs={{0,4},{4,8},{8,12},{12,0},{1,5},{5,9},{9,13},{13,1},{2,6},{6,10},{... | collective-permute-start | bytes 1474568 | tf_op jit(solution)/shard_map/ppermute | solution.py:39
  141.8 7.8 %collective-permute-done.15.refs_6_ = bf16[3,640,128]{2,1,0:T(8,128)(2,1)} collective-permute-done((bf16[3,640,128]{2,1,0:T(8,128)(2,1)S(1)}, bf16[3,640,128]{2,1,0:T(8,128)(2,1)}, u32[]{:S(2)}, u32[]{:S(2)}) %collective-permute-start.15) | collective-permute-done | bytes 491552 | tf_op jit(solution)/shard_map/ppermute | solution.py:39
  149.6 18.8 %collective-permute-done.17.refs_8_ = bf16[3,640,128]{2,1,0:T(8,128)(2,1)} collective-permute-done((bf16[3,640,128]{2,1,0:T(8,128)(2,1)S(1)}, bf16[3,640,128]{2,1,0:T(8,128)(2,1)}, u32[]{:S(2)}, u32[]{:S(2)}) %collective-permute-start.17) | collective-permute-done | bytes 491552 | tf_op jit(solution)/shard_map/ppermute | solution.py:39
  172.3 17.0 %collective-permute-done.19.refs_10_ = bf16[3,640,128]{2,1,0:T(8,128)(2,1)} collective-permute-done((bf16[3,640,128]{2,1,0:T(8,128)(2,1)S(1)}, bf16[3,640,128]{2,1,0:T(8,128)(2,1)}, u32[]{:S(2)}, u32[]{:S(2)}) %collective-permute-start.19) | collective-permute-done | bytes 491552 | tf_op jit(solution)/shard_map/ppermute | solution.py:39
  192.5 18.6 %collective-permute-done.34.refs_8_ = bf16[3,640,128]{2,1,0:T(8,128)(2,1)} collective-permute-done((bf16[3,640,128]{2,1,0:T(8,128)(2,1)}, bf16[3,640,128]{2,1,0:T(8,128)(2,1)}, u32[]{:S(2)}, u32[]{:S(2)}) %collective-permute-start.34) | collective-permute-done | bytes 491552 | tf_op jit(solution)/shard_map/ppermute | solution.py:39
  214.5 12.8 %collective-permute-done.36.refs_10_ = bf16[3,640,128]{2,1,0:T(8,128)(2,1)} collective-permute-done((bf16[3,640,128]{2,1,0:T(8,128)(2,1)}, bf16[3,640,128]{2,1,0:T(8,128)(2,1)}, u32[]{:S(2)}, u32[]{:S(2)}) %collective-permute-start.36) | collective-permute-done | bytes 491552 | tf_op jit(solution)/shard_map/ppermute | solution.py:39
  237.3 6.7 %shard_map.96.refs_0_ = bf16[768,2560]{1,0:T(8,128)(2,1)} custom-call(s32[1]{0:T(128)} %bitcast.4.b_ref, s32[4]{0:T(128)} %pad_add_fusion.3.at_ref, s32[2]{0:T(128)} %cfg_ref.7, bf16[768,2560]{1,0:T(8,128)(2,1)} %get-tuple-element.23.own_ref, bf16[768,2560]{1,0:T(8,128)(2,1)} %collective-permute-done.6.main_ref, f32[1,5120]{1,0:T(1,128)} %gain_ref.3, ...), custom_call_target="tpu_custom_call" | custom-call | flops 3932160 | bytes 11796480 | tf_op jit(solution)/shard_map/pallas_call | solution.py:115
  244.0 6.7 %shard_map.98.refs_1_ = bf16[768,2560]{1,0:T(8,128)(2,1)} custom-call(s32[1]{0:T(128)} %bitcast.4.b_ref, s32[4]{0:T(128)} %pad_add_fusion.4.at_ref, s32[2]{0:T(128)} %cfg_ref.7, bf16[768,2560]{1,0:T(8,128)(2,1)} %get-tuple-element.25.own_ref, bf16[768,2560]{1,0:T(8,128)(2,1)} %collective-permute-done.13.main_ref, f32[1,5120]{1,0:T(1,128)} %gain_ref.3, ...), custom_call_target="tpu_custom_call" | custom-call | flops 3932160 | bytes 11796480 | tf_op jit(solution)/shard_map/pallas_call | solution.py:115
  256.5 10.0 %collective-permute-done.20.refs_11_ = bf16[3,640,128]{2,1,0:T(8,128)(2,1)} collective-permute-done((bf16[3,640,128]{2,1,0:T(8,128)(2,1)}, bf16[3,640,128]{2,1,0:T(8,128)(2,1)}, u32[]{:S(2)}, u32[]{:S(2)}) %collective-permute-start.20) | collective-permute-done | bytes 491552 | tf_op jit(solution)/shard_map/ppermute | solution.py:34
  268.5 14.2 %project.3 = (bf16[2,768,128]{2,1,0:T(8,128)(2,1)}, bf16[2,768,256]{2,1,0:T(8,128)(2,1)}) custom-call(s32[5]{0:T(128)} %pad_add_fusion.2.place_ref, bf16[768,2560]{1,0:T(8,128)(2,1)} %shard_map.96.refs_0_, bf16[768,2560]{1,0:T(8,128)(2,1)} %shard_map.98.refs_1_, bf16[768,2560]{1,0:T(8,128)(2,1)} %get-tuple-element.26.refs_2_, ...), custom_call_target="tpu_custom_call" | custom-call | flops 6039797760 | bytes 20840448 | tf_op jit(solution)/shard_map/project/pallas_call | solution.py:158
  288.1 10.0 %collective-permute-done.37.refs_11_ = bf16[3,640,128]{2,1,0:T(8,128)(2,1)} collective-permute-done((bf16[3,640,128]{2,1,0:T(8,128)(2,1)}, bf16[3,640,128]{2,1,0:T(8,128)(2,1)}, u32[]{:S(2)}, u32[]{:S(2)}) %collective-permute-start.37) | collective-permute-done | bytes 491552 | tf_op jit(solution)/shard_map/ppermute | solution.py:34
  298.6 14.1 %project.4 = (bf16[2,768,128]{2,1,0:T(8,128)(2,1)}, bf16[2,768,256]{2,1,0:T(8,128)(2,1)}) custom-call(s32[5]{0:T(128)} %pad_add_fusion.2.place_ref, bf16[768,2560]{1,0:T(8,128)(2,1)} %shard_map.96.refs_0_, bf16[768,2560]{1,0:T(8,128)(2,1)} %shard_map.98.refs_1_, bf16[768,2560]{1,0:T(8,128)(2,1)} %get-tuple-element.26.refs_2_, ...), custom_call_target="tpu_custom_call" | custom-call | flops 6039797760 | bytes 20840448 | tf_op jit(solution)/shard_map/project/pallas_call | solution.py:158
  319.1 10.5 %collective-permute-done.52.refs_11_ = bf16[3,640,128]{2,1,0:T(8,128)(2,1)S(1)} collective-permute-done((bf16[3,640,128]{2,1,0:T(8,128)(2,1)}, bf16[3,640,128]{2,1,0:T(8,128)(2,1)S(1)}, u32[]{:S(2)}, u32[]{:S(2)}) %collective-permute-start.52) | collective-permute-done | bytes 491552 | tf_op jit(solution)/shard_map/ppermute | solution.py:34
  330.4 14.2 %project.5 = (bf16[2,768,128]{2,1,0:T(8,128)(2,1)}, bf16[2,768,256]{2,1,0:T(8,128)(2,1)}) custom-call(s32[5]{0:T(128)} %pad_add_fusion.2.place_ref, bf16[768,2560]{1,0:T(8,128)(2,1)} %shard_map.96.refs_0_, bf16[768,2560]{1,0:T(8,128)(2,1)} %shard_map.98.refs_1_, bf16[768,2560]{1,0:T(8,128)(2,1)} %get-tuple-element.26.refs_2_, ...), custom_call_target="tpu_custom_call" | custom-call | flops 6039797760 | bytes 20840448 | tf_op jit(solution)/shard_map/project/pallas_call | solution.py:158
  346.6 7.3 %attend.3 = (bf16[1152,128]{1,0:T(8,128)(2,1)}, bf16[384,128]{1,0:T(8,128)(2,1)}) custom-call(s32[1]{0:T(128)} %bitcast.4.b_ref, bf16[2,768,128]{2,1,0:T(8,128)(2,1)} %get-tuple-element.28.q_ref, bf16[2,768,256]{2,1,0:T(8,128)(2,1)} %get-tuple-element.29.own_ref, bf16[2,768,256]{2,1,0:T(8,128)(2,1)} %collective-permute-done.21.other_ref), custom_call_target="tpu_custom_call" | custom-call | flops 1207959552 | bytes 2359296 | tf_op jit(solution)/shard_map/attend/pallas_call | solution.py:227
  355.2 8.2 %collective-permute-done.38.other_ref = bf16[2,768,256]{2,1,0:T(8,128)(2,1)} collective-permute-done((bf16[2,768,256]{2,1,0:T(8,128)(2,1)}, bf16[2,768,256]{2,1,0:T(8,128)(2,1)}, u32[]{:S(2)}, u32[]{:S(2)}) %collective-permute-start.38) | collective-permute-done | bytes 786464 | tf_op jit(solution)/shard_map/ppermute | solution.py:34
  363.4 7.3 %attend.4 = (bf16[1152,128]{1,0:T(8,128)(2,1)}, bf16[384,128]{1,0:T(8,128)(2,1)}) custom-call(s32[1]{0:T(128)} %bitcast.4.b_ref, bf16[2,768,128]{2,1,0:T(8,128)(2,1)} %get-tuple-element.32.q_ref, bf16[2,768,256]{2,1,0:T(8,128)(2,1)} %get-tuple-element.33.own_ref, bf16[2,768,256]{2,1,0:T(8,128)(2,1)} %collective-permute-done.38.other_ref), custom_call_target="tpu_custom_call" | custom-call | flops 1207959552 | bytes 2359296 | tf_op jit(solution)/shard_map/attend/pallas_call | solution.py:227
  378.7 7.3 %attend.5 = (bf16[1152,128]{1,0:T(8,128)(2,1)}, bf16[384,128]{1,0:T(8,128)(2,1)}) custom-call(s32[1]{0:T(128)} %bitcast.4.b_ref, bf16[2,768,128]{2,1,0:T(8,128)(2,1)} %get-tuple-element.36.q_ref, bf16[2,768,256]{2,1,0:T(8,128)(2,1)} %get-tuple-element.37.own_ref, bf16[2,768,256]{2,1,0:T(8,128)(2,1)} %copy-done.30), custom_call_target="tpu_custom_call" | custom-call | flops 1207959552 | bytes 2359296 | tf_op jit(solution)/shard_map/attend/pallas_call | solution.py:227
  394.7 12.1 %collective-permute-start.42 = (bf16[1152,128]{1,0:T(8,128)(2,1)S(1)}, bf16[1152,128]{1,0:T(8,128)(2,1)S(1)}, u32[]{:S(2)}, u32[]{:S(2)}) collective-permute-start(bf16[1152,128]{1,0:T(8,128)(2,1)S(1)} %select_dynamic-update-slice_fusion.1.refs_0_), channel_id=1, source_target_pairs={{0,12},{4,0},{8,4},{12,8},{1,13},{5,1},{9,5},{13,9},{2,14},{6,2},{... | collective-permute-start | bytes 884744 | tf_op jit(solution)/shard_map/ppermute | solution.py:39
  413.5 6.4 %collective-permute-done.40.refs_1_ = bf16[1152,128]{1,0:T(8,128)(2,1)S(1)} collective-permute-done((bf16[1152,128]{1,0:T(8,128)(2,1)S(1)}, bf16[1152,128]{1,0:T(8,128)(2,1)S(1)}, u32[]{:S(2)}, u32[]{:S(2)}) %collective-permute-start.40) | collective-permute-done | bytes 294944 | tf_op jit(solution)/shard_map/ppermute | solution.py:39
  419.9 9.8 %collective-permute-done.41.refs_2_ = bf16[1152,128]{1,0:T(8,128)(2,1)S(1)} collective-permute-done((bf16[1152,128]{1,0:T(8,128)(2,1)S(1)}, bf16[1152,128]{1,0:T(8,128)(2,1)S(1)}, u32[]{:S(2)}, u32[]{:S(2)}) %collective-permute-start.41) | collective-permute-done | bytes 294944 | tf_op jit(solution)/shard_map/ppermute | solution.py:39
  437.8 7.4 %collective-permute-done.55.refs_9_ = bf16[1152,128]{1,0:T(8,128)(2,1)S(1)} collective-permute-done((bf16[1152,128]{1,0:T(8,128)(2,1)}, bf16[1152,128]{1,0:T(8,128)(2,1)S(1)}, u32[]{:S(2)}, u32[]{:S(2)}) %collective-permute-start.55) | collective-permute-done | bytes 294944 | tf_op jit(solution)/shard_map/ppermute | solution.py:39
  488.1 7.0 %project_out.4.refs_16_ = f32[768,640]{1,0:T(8,128)} custom-call(s32[5]{0:T(128)} %pad_add_fusion.1.at_ref, bf16[1152,128]{1,0:T(8,128)(2,1)} %copy-done.4, bf16[1152,128]{1,0:T(8,128)(2,1)} %copy-done.7, bf16[1152,128]{1,0:T(8,128)(2,1)} %copy-done.8, bf16[1152,128]{1,0:T(8,128)(2,1)} %copy-done.9, bf16[1152,128]{1,0:T(8,128)(2,1)} %copy-done.10, ...), custom_call_target="tpu_custom_call" | custom-call | flops 2013265920 | bytes 9699328 | tf_op jit(solution)/shard_map/project_out/pallas_call | solution.py:293
  525.5 9.8 %collective-permute-start.66 = (bf16[2,192,640]{2,1,0:T(8,128)(2,1)S(1)}, bf16[2,192,640]{2,1,0:T(8,128)(2,1)S(1)}, u32[]{:S(2)}, u32[]{:S(2)}) collective-permute-start(bf16[2,192,640]{2,1,0:T(8,128)(2,1)S(1)} %get-tuple-element.58), channel_id=1, source_target_pairs={{0,0},{1,4},{4,1},{5,5},{8,16},{9,20},{12,17},{13,21},{16,8},{17,1... | collective-permute-start | bytes 1474568 | tf_op jit(solution)/shard_map/ppermute | solution.py:425
  535.4 7.3 %collective-permute-done.65 = bf16[2,192,640]{2,1,0:T(8,128)(2,1)S(1)} collective-permute-done((bf16[2,192,640]{2,1,0:T(8,128)(2,1)S(1)}, bf16[2,192,640]{2,1,0:T(8,128)(2,1)S(1)}, u32[]{:S(2)}, u32[]{:S(2)}) %collective-permute-start.65) | collective-permute-done | bytes 491552 | tf_op jit(solution)/shard_map/ppermute | solution.py:425
  542.6 13.2 %collective-permute-done.66 = bf16[2,192,640]{2,1,0:T(8,128)(2,1)S(1)} collective-permute-done((bf16[2,192,640]{2,1,0:T(8,128)(2,1)S(1)}, bf16[2,192,640]{2,1,0:T(8,128)(2,1)S(1)}, u32[]{:S(2)}, u32[]{:S(2)}) %collective-permute-start.66) | collective-permute-done | bytes 491552 | tf_op jit(solution)/shard_map/ppermute | solution.py:425
  (201 shorter events, 202.4 us)
Async XLA Ops:
  38.4 27.8 %collective-permute-start.7 = (bf16[192,2560]{1,0:T(8,128)(2,1)S(1)}, bf16[192,2560]{1,0:T(8,128)(2,1)S(1)}, u32[]{:S(2)}, u32[]{:S(2)}) collective-permute-start(bf16[192,2560]{1,0:T(8,128)(2,1)S(1)} %collective-permute-done.refs_1_), channel_id=1, source_target_pairs={{0,1},{1,0},{4,5},{5,4},{8,9},{9,8},{2,3},{3,2},{6,7},{7,6},{10,11... | collective-permute-start | bytes 2949128 | tf_op jit(solution)/shard_map/ppermute | solution.py:363
  62.1 28.9 %collective-permute-start.12 = (bf16[192,2560]{1,0:T(8,128)(2,1)S(1)}, bf16[192,2560]{1,0:T(8,128)(2,1)}, u32[]{:S(2)}, u32[]{:S(2)}) collective-permute-start(bf16[192,2560]{1,0:T(8,128)(2,1)S(1)} %collective-permute-done.1.refs_6_), channel_id=1, source_target_pairs={{4,5},{5,4},{8,9},{9,8},{12,13},{13,12},{6,7},{7,6},{10,11},{11,10... | collective-permute-start | bytes 2949128 | tf_op jit(solution)/shard_map/ppermute | solution.py:362
  64.5 29.6 %collective-permute-start.9 = (bf16[192,2560]{1,0:T(8,128)(2,1)}, bf16[192,2560]{1,0:T(8,128)(2,1)}, u32[]{:S(2)}, u32[]{:S(2)}) collective-permute-start(bf16[192,2560]{1,0:T(8,128)(2,1)} %collective-permute-done.4.refs_3_), channel_id=1, source_target_pairs={{0,1},{1,0},{4,5},{5,4},{2,3},{3,2},{6,7},{7,6},{16,17},{17,16},{2... | collective-permute-start | bytes 2949128 | tf_op jit(solution)/shard_map/ppermute | solution.py:363
  66.2 40.5 %collective-permute-start.10 = (bf16[192,2560]{1,0:T(8,128)(2,1)S(1)}, bf16[192,2560]{1,0:T(8,128)(2,1)}, u32[]{:S(2)}, u32[]{:S(2)}) collective-permute-start(bf16[192,2560]{1,0:T(8,128)(2,1)S(1)} %collective-permute-done.2.refs_4_), channel_id=1, source_target_pairs={{8,9},{9,8},{12,13},{13,12},{10,11},{11,10},{14,15},{15,14},{24,25... | collective-permute-start | bytes 2949128 | tf_op jit(solution)/shard_map/ppermute | solution.py:362
  78.8 27.9 %collective-permute-start.8 = (bf16[192,2560]{1,0:T(8,128)(2,1)}, bf16[192,2560]{1,0:T(8,128)(2,1)}, u32[]{:S(2)}, u32[]{:S(2)}) collective-permute-start(bf16[192,2560]{1,0:T(8,128)(2,1)} %collective-permute-done.3.refs_2_), channel_id=1, source_target_pairs={{12,13},{13,12},{14,15},{15,14},{28,29},{29,28},{30,31},{31,30}} | collective-permute-start | bytes 2949128 | tf_op jit(solution)/shard_map/ppermute | solution.py:362
  91.1 140.5 %collective-permute-start.6 = (bf16[768,2560]{1,0:T(8,128)(2,1)}, bf16[768,2560]{1,0:T(8,128)(2,1)}, u32[]{:S(2)}, u32[]{:S(2)}) collective-permute-start(bf16[768,2560]{1,0:T(8,128)(2,1)} %get-tuple-element.23.own_ref), channel_id=1, source_target_pairs={{0,16},{1,17},{2,18},{3,19},{4,20},{5,21},{6,22},{7,23},{8,24},{9,... | collective-permute-start | bytes 11796488 | tf_op jit(solution)/shard_map/ppermute | solution.py:375
  114.3 118.7 %collective-permute-start.13 = (bf16[768,2560]{1,0:T(8,128)(2,1)}, bf16[768,2560]{1,0:T(8,128)(2,1)}, u32[]{:S(2)}, u32[]{:S(2)}) collective-permute-start(bf16[768,2560]{1,0:T(8,128)(2,1)} %get-tuple-element.25.own_ref), channel_id=1, source_target_pairs={{0,16},{1,17},{2,18},{3,19},{4,20},{5,21},{6,22},{7,23},{8,24},{9,... | collective-permute-start | bytes 11796488 | tf_op jit(solution)/shard_map/ppermute | solution.py:375
  121.5 28.1 %collective-permute-start.15 = (bf16[3,640,128]{2,1,0:T(8,128)(2,1)S(1)}, bf16[3,640,128]{2,1,0:T(8,128)(2,1)}, u32[]{:S(2)}, u32[]{:S(2)}) collective-permute-start(bf16[3,640,128]{2,1,0:T(8,128)(2,1)S(1)} %get-tuple-element.51), channel_id=1, source_target_pairs={{0,4},{4,8},{8,12},{12,0},{1,5},{5,9},{9,13},{13,1},{2,6},{6,10},{... | collective-permute-start | bytes 1474568 | tf_op jit(solution)/shard_map/ppermute | solution.py:39
  141.3 89.7 %collective-permute-start.30 = (bf16[1536,640]{1,0:T(8,128)(2,1)S(1)}, bf16[1536,640]{1,0:T(8,128)(2,1)}, u32[]{:S(2)}, u32[]{:S(2)}) collective-permute-start(bf16[1536,640]{1,0:T(8,128)(2,1)S(1)} %bitcast.59), channel_id=1, source_target_pairs={{0,2},{2,0},{1,3},{3,1},{4,6},{6,4},{5,7},{7,5},{8,10},{10,8},{9,1... | collective-permute-start | bytes 5898248 | tf_op jit(solution)/shard_map/ppermute | solution.py:34
  149.6 39.7 %collective-permute-start.19 = (bf16[3,640,128]{2,1,0:T(8,128)(2,1)S(1)}, bf16[3,640,128]{2,1,0:T(8,128)(2,1)}, u32[]{:S(2)}, u32[]{:S(2)}) collective-permute-start(bf16[3,640,128]{2,1,0:T(8,128)(2,1)S(1)} %get-tuple-element.49), channel_id=1, source_target_pairs={{0,12},{4,0},{8,4},{12,8},{1,13},{5,1},{9,5},{13,9},{2,14},{6,2},{... | collective-permute-start | bytes 1474568 | tf_op jit(solution)/shard_map/ppermute | solution.py:39
  192.0 75.0 %collective-permute-start.14 = (bf16[3,640,384]{2,1,0:T(8,128)(2,1)}, bf16[3,640,384]{2,1,0:T(8,128)(2,1)S(1)}, u32[]{:S(2)}, u32[]{:S(2)}) collective-permute-start(bf16[3,640,384]{2,1,0:T(8,128)(2,1)} %dynamic-slice_bitcast_fusion), channel_id=1, source_target_pairs={{0,2},{2,0},{1,3},{3,1},{4,6},{6,4},{5,7},{7,5},{8,10},{10,8},{9,1... | collective-permute-start | bytes 4423688 | tf_op jit(solution)/shard_map/ppermute | solution.py:34
  233.1 33.4 %collective-permute-start.20 = (bf16[3,640,128]{2,1,0:T(8,128)(2,1)}, bf16[3,640,128]{2,1,0:T(8,128)(2,1)}, u32[]{:S(2)}, u32[]{:S(2)}) collective-permute-start(bf16[3,640,128]{2,1,0:T(8,128)(2,1)} %collective-permute-done.19.refs_10_), channel_id=1, source_target_pairs={{0,2},{2,0},{1,3},{3,1},{4,6},{6,4},{5,7},{7,5},{8,10},{10,8},{9,1... | collective-permute-start | bytes 1474568 | tf_op jit(solution)/shard_map/ppermute | solution.py:34
  250.7 32.0 %collective-permute-start.49 = (bf16[3,640,128]{2,1,0:T(8,128)(2,1)}, bf16[3,640,128]{2,1,0:T(8,128)(2,1)}, u32[]{:S(2)}, u32[]{:S(2)}) collective-permute-start(bf16[3,640,128]{2,1,0:T(8,128)(2,1)} %get-tuple-element.52), channel_id=1, source_target_pairs={{0,8},{4,12},{8,0},{12,4},{1,9},{5,13},{9,1},{13,5},{2,10},{6,14},... | collective-permute-start | bytes 1474568 | tf_op jit(solution)/shard_map/ppermute | solution.py:39
  250.7 33.2 %collective-permute-start.51 = (bf16[3,640,128]{2,1,0:T(8,128)(2,1)}, bf16[3,640,128]{2,1,0:T(8,128)(2,1)}, u32[]{:S(2)}, u32[]{:S(2)}) collective-permute-start(bf16[3,640,128]{2,1,0:T(8,128)(2,1)} %get-tuple-element.44), channel_id=1, source_target_pairs={{0,12},{4,0},{8,4},{12,8},{1,13},{5,1},{9,5},{13,9},{2,14},{6,2},{... | collective-permute-start | bytes 1474568 | tf_op jit(solution)/shard_map/ppermute | solution.py:39
  256.0 28.9 %collective-permute-start.33 = (bf16[3,640,128]{2,1,0:T(8,128)(2,1)}, bf16[3,640,128]{2,1,0:T(8,128)(2,1)}, u32[]{:S(2)}, u32[]{:S(2)}) collective-permute-start(bf16[3,640,128]{2,1,0:T(8,128)(2,1)} %collective-permute-done.32.refs_6_), channel_id=1, source_target_pairs={{0,2},{2,0},{1,3},{3,1},{4,6},{6,4},{5,7},{7,5},{8,10},{10,8},{9,1... | collective-permute-start | bytes 1474568 | tf_op jit(solution)/shard_map/ppermute | solution.py:34
  267.0 31.1 %collective-permute-start.37 = (bf16[3,640,128]{2,1,0:T(8,128)(2,1)}, bf16[3,640,128]{2,1,0:T(8,128)(2,1)}, u32[]{:S(2)}, u32[]{:S(2)}) collective-permute-start(bf16[3,640,128]{2,1,0:T(8,128)(2,1)} %collective-permute-done.36.refs_10_), channel_id=1, source_target_pairs={{0,2},{2,0},{1,3},{3,1},{4,6},{6,4},{5,7},{7,5},{8,10},{10,8},{9,1... | collective-permute-start | bytes 1474568 | tf_op jit(solution)/shard_map/ppermute | solution.py:34
  282.7 30.0 %collective-permute-start.48 = (bf16[3,640,128]{2,1,0:T(8,128)(2,1)}, bf16[3,640,128]{2,1,0:T(8,128)(2,1)S(1)}, u32[]{:S(2)}, u32[]{:S(2)}) collective-permute-start(bf16[3,640,128]{2,1,0:T(8,128)(2,1)} %collective-permute-done.47.refs_6_), channel_id=1, source_target_pairs={{0,2},{2,0},{1,3},{3,1},{4,6},{6,4},{5,7},{7,5},{8,10},{10,8},{9,1... | collective-permute-start | bytes 1474568 | tf_op jit(solution)/shard_map/ppermute | solution.py:34
  283.9 35.1 %collective-permute-start.50 = (bf16[3,640,128]{2,1,0:T(8,128)(2,1)}, bf16[3,640,128]{2,1,0:T(8,128)(2,1)S(1)}, u32[]{:S(2)}, u32[]{:S(2)}) collective-permute-start(bf16[3,640,128]{2,1,0:T(8,128)(2,1)} %collective-permute-done.49.refs_8_), channel_id=1, source_target_pairs={{0,2},{2,0},{1,3},{3,1},{4,6},{6,4},{5,7},{7,5},{8,10},{10,8},{9,1... | collective-permute-start | bytes 1474568 | tf_op jit(solution)/shard_map/ppermute | solution.py:34
  284.8 44.8 %collective-permute-start.52 = (bf16[3,640,128]{2,1,0:T(8,128)(2,1)}, bf16[3,640,128]{2,1,0:T(8,128)(2,1)S(1)}, u32[]{:S(2)}, u32[]{:S(2)}) collective-permute-start(bf16[3,640,128]{2,1,0:T(8,128)(2,1)} %collective-permute-done.51.refs_10_), channel_id=1, source_target_pairs={{0,2},{2,0},{1,3},{3,1},{4,6},{6,4},{5,7},{7,5},{8,10},{10,8},{9,1... | collective-permute-start | bytes 1474568 | tf_op jit(solution)/shard_map/ppermute | solution.py:34
  287.6 98.5 %collective-permute-start.31 = (bf16[1536,640]{1,0:T(8,128)(2,1)}, bf16[1536,640]{1,0:T(8,128)(2,1)}, u32[]{:S(2)}, u32[]{:S(2)}) collective-permute-start(bf16[1536,640]{1,0:T(8,128)(2,1)} %get-tuple-element.53), channel_id=1, source_target_pairs={{0,1},{1,0},{2,3},{3,2},{4,5},{5,4},{6,7},{7,6},{8,9},{9,8},{10,11... | collective-permute-start | bytes 5898248 | tf_op jit(solution)/shard_map/ppermute | solution.py:34
  298.1 48.5 %collective-permute-start.21 = (bf16[2,768,256]{2,1,0:T(8,128)(2,1)}, bf16[2,768,256]{2,1,0:T(8,128)(2,1)}, u32[]{:S(2)}, u32[]{:S(2)}) collective-permute-start(bf16[2,768,256]{2,1,0:T(8,128)(2,1)} %get-tuple-element.29.own_ref), channel_id=1, source_target_pairs={{0,2},{2,0},{1,3},{3,1},{4,6},{6,4},{5,7},{7,5},{8,10},{10,8},{9,1... | collective-permute-start | bytes 2359304 | tf_op jit(solution)/shard_map/ppermute | solution.py:34
  312.7 50.7 %collective-permute-start.38 = (bf16[2,768,256]{2,1,0:T(8,128)(2,1)}, bf16[2,768,256]{2,1,0:T(8,128)(2,1)}, u32[]{:S(2)}, u32[]{:S(2)}) collective-permute-start(bf16[2,768,256]{2,1,0:T(8,128)(2,1)} %get-tuple-element.33.own_ref), channel_id=1, source_target_pairs={{0,2},{2,0},{1,3},{3,1},{4,6},{6,4},{5,7},{7,5},{8,10},{10,8},{9,1... | collective-permute-start | bytes 2359304 | tf_op jit(solution)/shard_map/ppermute | solution.py:34
  344.6 33.2 %collective-permute-start.53 = (bf16[2,768,256]{2,1,0:T(8,128)(2,1)}, bf16[2,768,256]{2,1,0:T(8,128)(2,1)S(1)}, u32[]{:S(2)}, u32[]{:S(2)}) collective-permute-start(bf16[2,768,256]{2,1,0:T(8,128)(2,1)} %get-tuple-element.37.own_ref), channel_id=1, source_target_pairs={{0,2},{2,0},{1,3},{3,1},{4,6},{6,4},{5,7},{7,5},{8,10},{10,8},{9,1... | collective-permute-start | bytes 2359304 | tf_op jit(solution)/shard_map/ppermute | solution.py:34
  377.8 32.8 %collective-permute-start.25 = (bf16[1152,128]{1,0:T(8,128)(2,1)S(1)}, bf16[1152,128]{1,0:T(8,128)(2,1)}, u32[]{:S(2)}, u32[]{:S(2)}) collective-permute-start(bf16[1152,128]{1,0:T(8,128)(2,1)S(1)} %select_dynamic-update-slice_fusion.2.refs_0_), channel_id=1, source_target_pairs={{0,12},{4,0},{8,4},{12,8},{1,13},{5,1},{9,5},{13,9},{2,14},{6,2},{... | collective-permute-start | bytes 884744 | tf_op jit(solution)/shard_map/ppermute | solution.py:39
  389.4 30.5 %collective-permute-start.40 = (bf16[1152,128]{1,0:T(8,128)(2,1)S(1)}, bf16[1152,128]{1,0:T(8,128)(2,1)S(1)}, u32[]{:S(2)}, u32[]{:S(2)}) collective-permute-start(bf16[1152,128]{1,0:T(8,128)(2,1)S(1)} %select_dynamic-update-slice_fusion.1.refs_0_), channel_id=1, source_target_pairs={{0,4},{4,8},{8,12},{12,0},{1,5},{5,9},{9,13},{13,1},{2,6},{6,10},{... | collective-permute-start | bytes 884744 | tf_op jit(solution)/shard_map/ppermute | solution.py:39
  394.7 35.0 %collective-permute-start.41 = (bf16[1152,128]{1,0:T(8,128)(2,1)S(1)}, bf16[1152,128]{1,0:T(8,128)(2,1)S(1)}, u32[]{:S(2)}, u32[]{:S(2)}) collective-permute-start(bf16[1152,128]{1,0:T(8,128)(2,1)S(1)} %select_dynamic-update-slice_fusion.1.refs_0_), channel_id=1, source_target_pairs={{0,8},{4,12},{8,0},{12,4},{1,9},{5,13},{9,1},{13,5},{2,10},{6,14},... | collective-permute-start | bytes 884744 | tf_op jit(solution)/shard_map/ppermute | solution.py:39
  394.7 41.3 %collective-permute-start.42 = (bf16[1152,128]{1,0:T(8,128)(2,1)S(1)}, bf16[1152,128]{1,0:T(8,128)(2,1)S(1)}, u32[]{:S(2)}, u32[]{:S(2)}) collective-permute-start(bf16[1152,128]{1,0:T(8,128)(2,1)S(1)} %select_dynamic-update-slice_fusion.1.refs_0_), channel_id=1, source_target_pairs={{0,12},{4,0},{8,4},{12,8},{1,13},{5,1},{9,5},{13,9},{2,14},{6,2},{... | collective-permute-start | bytes 884744 | tf_op jit(solution)/shard_map/ppermute | solution.py:39
  412.8 32.4 %collective-permute-start.55 = (bf16[1152,128]{1,0:T(8,128)(2,1)}, bf16[1152,128]{1,0:T(8,128)(2,1)S(1)}, u32[]{:S(2)}, u32[]{:S(2)}) collective-permute-start(bf16[1152,128]{1,0:T(8,128)(2,1)} %select_dynamic-update-slice_fusion.refs_8_), channel_id=1, source_target_pairs={{0,4},{4,8},{8,12},{12,0},{1,5},{5,9},{9,13},{13,1},{2,6},{6,10},{... | collective-permute-start | bytes 884744 | tf_op jit(solution)/shard_map/ppermute | solution.py:39
  419.9 26.6 %collective-permute-start.56 = (bf16[1152,128]{1,0:T(8,128)(2,1)}, bf16[1152,128]{1,0:T(8,128)(2,1)S(1)}, u32[]{:S(2)}, u32[]{:S(2)}) collective-permute-start(bf16[1152,128]{1,0:T(8,128)(2,1)} %select_dynamic-update-slice_fusion.refs_8_), channel_id=1, source_target_pairs={{0,8},{4,12},{8,0},{12,4},{1,9},{5,13},{9,1},{13,5},{2,10},{6,14},... | collective-permute-start | bytes 884744 | tf_op jit(solution)/shard_map/ppermute | solution.py:39
  436.5 76.3 %collective-permute-start.63 = (bf16[1536,640]{1,0:T(8,128)(2,1)S(1)}, bf16[1536,640]{1,0:T(8,128)(2,1)}, u32[]{:S(2)}, u32[]{:S(2)}) collective-permute-start(bf16[1536,640]{1,0:T(8,128)(2,1)S(1)} %get-tuple-element.54.refs_16_.refs_17_.refs_18_.refs_19_.refs_24_.refs_25_.refs_26_.refs_27_.refs_8_.refs_9_.re, ...), channel_id=1, source_target_pairs={{16,0},{17,1},{18,2},{19,3},{20,4},{21,5},{22,6},{23,7},{24,8},{25... | collective-permute-start | bytes 5898248 | tf_op jit(solution)/shard_map/ppermute | solution.py:388
  445.2 67.6 %collective-permute-start.64 = (bf16[1536,640]{1,0:T(8,128)(2,1)}, bf16[1536,640]{1,0:T(8,128)(2,1)}, u32[]{:S(2)}, u32[]{:S(2)}) collective-permute-start(bf16[1536,640]{1,0:T(8,128)(2,1)} %collective-permute-done.31.refs_20_.refs_21_.refs_22_.refs_23_.refs_28_.refs_29_.refs_30_.refs_31_.refs_12_.refs_13_.re, ...), channel_id=1, source_target_pairs={{16,0},{17,1},{18,2},{19,3},{20,4},{21,5},{22,6},{23,7},{24,8},{25... | collective-permute-start | bytes 5898248 | tf_op jit(solution)/shard_map/ppermute | solution.py:388
  525.5 30.3 %collective-permute-start.66 = (bf16[2,192,640]{2,1,0:T(8,128)(2,1)S(1)}, bf16[2,192,640]{2,1,0:T(8,128)(2,1)S(1)}, u32[]{:S(2)}, u32[]{:S(2)}) collective-permute-start(bf16[2,192,640]{2,1,0:T(8,128)(2,1)S(1)} %get-tuple-element.58), channel_id=1, source_target_pairs={{0,0},{1,4},{4,1},{5,5},{8,16},{9,20},{12,17},{13,21},{16,8},{17,1... | collective-permute-start | bytes 1474568 | tf_op jit(solution)/shard_map/ppermute | solution.py:425
  (67 other events, 1610.8 us)
